TPU v7x, 256 devices: a whole 4x4x8 slice. The times are simulated.
256 devices in a mesh: row: 8 (over x, z_lo), col: 32 (over z_hi, y, core).
Axes of the slice: x: 4, y: 4, z: 8 (z_hi: 4, z_lo: 2; z = z_hi * 2 + z_lo), core: 2. Of those that a mesh axis runs over, the one named last changes fastest.
Arguments:
- layer_input: bfloat16 [40960, 3072], P(('row', 'col')), may hold values from -0.5 to 0.5
- queries: bfloat16 [40960, 128], P(('row', 'col')), may hold values from -7 to 7
- key_states: bfloat16 [40960, 128], P(('row', 'col')), may hold values from -7 to 7
- value_states: bfloat16 [40960, 128], P(('row', 'col')), may hold values from -6 to 6
- forward_out: bfloat16 [40960, 128], P(('row', 'col')), may hold values from -1.5 to 1.5
- out_grad: bfloat16 [40960, 128], P(('row', 'col')), may hold values from -12 to 12
- token_pos: int32 [40960], replicated, may hold values from 0 to 40959, as said below
- block_sample: int32 [320], replicated, may hold values from 0 to 39, never falling along the last dimension, each value on 1 to 32 neighbouring positions
Outputs:
- query_grad: bfloat16 [40960, 128], P(('row', 'col'))
- key_grad: bfloat16 [40960, 128], P(('row', 'col'))
- value_grad: bfloat16 [40960, 128], P(('row', 'col'))
- weight_grad: float32 [3072, 384], P('col')
Inputs may be any that keep to these rules, and one draw needn't show every extreme that they name: `token_pos`: each packed position appears in exactly one slot. `block_sample`: never falling along the blocks; every sample spans 1 to 32 blocks and one spans exactly 32.
All inputs are finite; a program needn't handle non-finite values.
Results may differ from a plain program's by a relative error of at most 0.019.
Values may be sent and summed in bfloat16 or wider, within the bound.
A program may use at most 64 MiB of HBM per device.

v0:
```python
import math

import jax
import jax.numpy as jnp
from jax import lax
from jax.sharding import Mesh
from jax.sharding import PartitionSpec as P

BLK = 128
COL = ("col_0", "col_1", "col_2")
ROW_COL = ("row", "col_0", "col_1", "col_2")


NEG_FILL = -1e30


def in_one_piece(arrays, axis, dim, along):
    both = jnp.concatenate(arrays, axis=along)
    out, at, gathered = (lax.all_gather(both, axis, axis=dim, tiled=True), 0, [])
    for a in arrays:
        gathered.append(lax.slice_in_dim(out, at, at + a.shape[along], axis=along))
        at += a.shape[along]
    return tuple(gathered)


def all_in_one(array, axis):
    leaves = jax.tree.leaves(array)
    order = sorted(range(len(leaves)), key=lambda k: -leaves[k].size)
    width = (1, *leaves[order[0]].shape)[-1]
    lines = [
        jnp.pad(leaves[k].reshape(-1), (0, -leaves[k].size % width)).reshape(-1, width)
        for k in order
    ]
    both, at, found = (lax.all_gather(jnp.concatenate(lines), axis), 0, {})
    for k, line in zip(order, lines):
        share = both[:, at : at + len(line)].reshape(len(both), -1)
        found[k] = share[:, : leaves[k].size].reshape(-1, *leaves[k].shape)
        at += len(line)
    numbers = iter(range(len(leaves)))
    return jax.tree.map(lambda _: found[next(numbers)], array)


def combined_by_axis(array, axes, combine):
    for axis in axes:
        pieces = all_in_one(array, axis)
        array = jax.tree.map(lambda part: part[0], pieces)
        for k in range(1, lax.axis_size(axis)):
            array = combine(array, jax.tree.map(lambda part: part[k], pieces))
    return array


def split_up(array, dim, devices):
    dims = array.shape
    blocks = array.reshape(*dims[:dim], devices, dims[dim] // devices, *dims[dim + 1 :])
    return jnp.moveaxis(blocks, dim, 0)


def sum_at_owner(array, axis, dim):
    blocks = split_up(array, dim, lax.axis_size(axis))
    arrived = lax.all_to_all(blocks, axis, split_axis=0, concat_axis=0, tiled=True)
    return arrived.astype(jnp.float32).sum(axis=0)


def side_by_side(arrays, axis, dim, along):
    both = jnp.concatenate(arrays, axis=along)
    out, at, gathered = (sum_at_owner(both, axis, dim), 0, [])
    for a in arrays:
        gathered.append(lax.slice_in_dim(out, at, at + a.shape[along], axis=along))
        at += a.shape[along]
    return tuple(gathered)


def from_everyone(array, axis):
    devices = lax.axis_size(axis)
    return lax.all_to_all(
        jnp.broadcast_to(array[None], (devices, *array.shape)), axis, 0, 0, tiled=True
    )


def taken_together(array, axis):
    everything = from_everyone(array, axis)
    return jnp.sum(everything.astype(jnp.float32), axis=0)


def sample_of(positions, block_sample):
    block_index = positions // BLK
    block_ids = jnp.arange(block_sample.shape[0], dtype=jnp.int32)
    matches = block_index[:, None] == block_ids[None, :]
    return jnp.sum(jnp.where(matches, block_sample[None, :], 0), axis=1)


def weight_term(layer_input, all_grads):
    return lax.dot_general(
        layer_input, all_grads, (((0,), (0,)), ((), ())), preferred_element_type=jnp.float32
    )


def local(
    layer_input, queries, key_states, value_states, forward_out, out_grad, token_pos, block_sample
):
    token_count = queries.shape[0]
    head_width = queries.shape[1]
    score_scale = 1.0 / math.sqrt(head_width)
    col_count = lax.axis_size(COL)
    row_count = lax.axis_size("row")
    row_id = lax.axis_index("row")
    col_id = lax.axis_index(COL)
    query_rows, grad_rows, output_rows = in_one_piece((queries, out_grad, forward_out), COL, 0, 1)
    key_rows, value_rows = in_one_piece((key_states, value_states), "row", 0, 1)
    query_count = query_rows.shape[0]
    block_rows = math.gcd(query_count, 512)
    block_count = query_count // block_rows
    query_pos = lax.dynamic_slice_in_dim(token_pos, row_id * query_count, query_count)
    key_pos = lax.dynamic_index_in_dim(
        token_pos.reshape(row_count, col_count, token_count), col_id, axis=1, keepdims=False
    ).reshape(-1)
    key_sample = sample_of(key_pos, block_sample)
    query_blocks = query_rows.reshape(block_count, block_rows, head_width)
    grad_blocks = grad_rows.reshape(block_count, block_rows, head_width)
    output_blocks = output_rows.reshape(block_count, block_rows, head_width)
    query_samples = lax.map(
        lambda pos_block: sample_of(pos_block, block_sample),
        query_pos.reshape(block_count, block_rows),
    )

    def masked_scores(query_block, sample_block):
        scores = (
            lax.dot_general(
                query_block, key_rows, (((1,), (1,)), ((), ())), preferred_element_type=jnp.float32
            )
            * score_scale
        )
        live_pairs = sample_block[:, None] == key_sample[None, :]
        return (jnp.where(live_pairs, scores, NEG_FILL), live_pairs)

    def local_stats(running, inputs):
        scores, live_pairs = masked_scores(inputs[0], inputs[1])
        peak_rows = jnp.max(scores, axis=1)
        row_sum = jnp.sum(jnp.where(live_pairs, jnp.exp(scores - peak_rows[:, None]), 0.0), axis=1)
        return (running, (peak_rows, row_sum))

    unused, (peak_local, total_local) = lax.scan(
        local_stats, jnp.zeros((), jnp.float32), (query_blocks, query_samples)
    )
    peak_local = peak_local.reshape(-1)
    total_local = total_local.reshape(-1)

    def combine_stats(left_stats, right_stats):
        joint_peak = jnp.maximum(left_stats[0], right_stats[0])
        joint_sum = left_stats[1] * jnp.exp(left_stats[0] - joint_peak) + right_stats[1] * jnp.exp(
            right_stats[0] - joint_peak
        )
        return (joint_peak, joint_sum)

    row_peak, row_total = combined_by_axis((peak_local, total_local), COL, combine_stats)

    def backward_block(running, inputs):
        key_acc, value_acc = running
        query_block, grad_block, output_block, sample_block, peak_block, total_block = inputs
        scores, live_pairs = masked_scores(query_block, sample_block)
        prob_rows = (
            jnp.where(live_pairs, jnp.exp(scores - peak_block[:, None]), 0.0) / total_block[:, None]
        )
        prob_low = prob_rows.astype(jnp.bfloat16)
        value_acc = value_acc + lax.dot_general(
            prob_low, grad_block, (((0,), (0,)), ((), ())), preferred_element_type=jnp.float32
        )
        prob_grad = lax.dot_general(
            grad_block, value_rows, (((1,), (1,)), ((), ())), preferred_element_type=jnp.float32
        )
        row_delta = jnp.sum(
            grad_block.astype(jnp.float32) * output_block.astype(jnp.float32), axis=1
        )
        score_grad = (prob_rows * (prob_grad - row_delta[:, None])).astype(jnp.bfloat16)
        query_part = jnp.dot(score_grad, key_rows, preferred_element_type=jnp.float32) * score_scale
        key_step = (
            lax.dot_general(
                score_grad,
                query_block,
                (((0,), (0,)), ((), ())),
                preferred_element_type=jnp.float32,
            )
            * score_scale
        )
        return ((key_acc + key_step, value_acc), query_part)

    zero_keys = jnp.zeros((key_rows.shape[0], head_width), jnp.float32)
    (key_part, value_part), query_parts = lax.scan(
        backward_block,
        (zero_keys, zero_keys),
        (
            query_blocks,
            grad_blocks,
            output_blocks,
            query_samples,
            row_peak.reshape(block_count, block_rows),
            row_total.reshape(block_count, block_rows),
        ),
    )
    query_grad = sum_at_owner(
        query_parts.reshape(query_count, head_width).astype(jnp.bfloat16), COL, 0
    ).astype(jnp.bfloat16)
    key_sum, value_sum = side_by_side(
        (key_part.astype(jnp.bfloat16), value_part.astype(jnp.bfloat16)), "row", 0, 1
    )
    key_grad = key_sum.astype(jnp.bfloat16)
    value_grad = value_sum.astype(jnp.bfloat16)
    all_grads = jnp.concatenate([query_grad, key_grad, value_grad], axis=1)
    weight_shard = lax.psum_scatter(
        weight_term(layer_input, all_grads).astype(jnp.bfloat16),
        COL,
        scatter_dimension=0,
        tiled=True,
    )
    weight_grad = taken_together(weight_shard, "row").astype(jnp.float32)
    return (query_grad, key_grad, value_grad, weight_grad)


def solution(mesh):
    finer = Mesh(
        mesh.devices.reshape(mesh.shape["row"], 4, 4, 2), ("row", "col_0", "col_1", "col_2")
    )
    return jax.shard_map(
        local,
        mesh=finer,
        in_specs=(
            P(ROW_COL, None),
            P(ROW_COL, None),
            P(ROW_COL, None),
            P(ROW_COL, None),
            P(ROW_COL, None),
            P(ROW_COL, None),
            P(),
            P(),
        ),
        out_specs=(P(ROW_COL, None), P(ROW_COL, None), P(ROW_COL, None), P(COL, None)),
        check_vma=False,
    )
```

profile of v0, /device:TPU:1, one launch (start us, length us, event | category | flops | bytes accessed | tf_op | source)
XLA Modules:
  0.0 390.8 jit_solution(9021515613493896246)
XLA Ops:
  7.2 1.6 pad_maximum_fusion.1
  12.6 27.6 %all_gather.25 = bf16[1280,256]{1,0:T(8,128)(2,1)S(1)} all-gather(bf16[160,256]{1,0:T(8,128)(2,1)S(1)} %pad_maximum_fusion.2), channel_id=1, replica_groups=mesh['row'=8,'col_0'=4,'col_1'=4,'col_2'=2] {'row'}, dimensions={0}, use_global_device_ids=true | all-gather | bytes 737280 | tf_op jit(solution)/shard_map/all_gather | solution.py:19
  40.2 2.8 while.39
  43.1 31.4 %all-gather.8.cloned.1.call-done = bf16[5120,384]{1,0:T(8,128)(2,1)} async-done(((bf16[160,384]{1,0:T(8,128)(2,1)}), bf16[5120,384]{1,0:T(8,128)(2,1)}) %all-gather.8.cloned.1.call-update) | async-done | bytes 3932176 | tf_op jit(solution)/shard_map/all_gather | solution.py:19
  74.5 4.0 %fusion.64 = (bf16[5120,128]{1,0:T(8,128)(2,1)}, bf16[5120,128]{1,0:T(8,128)(2,1)}, bf16[5120,128]{1,0:T(8,128)(2,1)}) fusion(bf16[5120,384]{1,0:T(8,128)(2,1)} %all-gather.8.cloned.1.call-done), kind=kLoop, calls=%fused_computation.120 | loop fusion | bytes 7864320 | tf_op jit(solution)/shard_map/slice | solution.py:21
  78.6 24.2 %while.40 = (s32[]{:T(128)}, f32[10,512]{1,0:T(8,128)S(1)}, f32[10,512]{1,0:T(8,128)S(1)}, s32[10,512]{1,0:T(8,128)S(1)}, s32[1280]{0:T(1024)S(1)}, /*index=5*/b...) while((s32[]{:T(128)}, f32[10,512]{1,0:T(8,128)S(1)}, ...), condition=%wide.region_7.8_spmd, body=%wide.region_4.7_spmd.sunk | while | flops 173014016 | bytes 5734517 | solution.py:142
  78.6 1.6 fusion.93
  81.0 1.6 fusion.93
  83.4 1.6 fusion.93
  85.9 1.6 fusion.93
  88.3 1.6 fusion.93
  90.7 1.6 fusion.93
  93.1 1.6 fusion.93
  95.6 1.6 fusion.93
  98.0 1.6 fusion.93
  100.4 1.6 fusion.93
  102.9 11.2 %all-gather.3 = f32[4,2,5120]{2,1,0:T(2,128)S(1)} all-gather(f32[1,2,5120]{2,1,0:T(2,128)S(1)} %maximum_bitcast_fusion), channel_id=2, replica_groups=mesh['row'=8,'col_0'=4,'col_1'=4,'col_2'=2] {'col_0'}, dimensions={0}, use_global_device_ids=true | all-gather | bytes 204800 | tf_op jit(solution)/shard_map/all_gather | solution.py:34
  114.4 10.0 %all-gather.4 = f32[4,2,5120]{2,1,0:T(2,128)S(1)} all-gather(f32[1,2,5120]{2,1,0:T(2,128)S(1)} %maximum_bitcast_fusion.1), channel_id=3, replica_groups=mesh['row'=8,'col_0'=4,'col_1'=4,'col_2'=2] {'col_1'}, dimensions={0}, use_global_device_ids=true | all-gather | bytes 204800 | tf_op jit(solution)/shard_map/all_gather | solution.py:34
  124.6 7.8 %all-gather.5 = f32[2,2,5120]{2,1,0:T(2,128)S(1)} all-gather(f32[1,2,5120]{2,1,0:T(2,128)S(1)} %maximum_bitcast_fusion.2), channel_id=4, replica_groups=mesh['row'=8,'col_0'=4,'col_1'=4,'col_2'=2] {'col_2'}, dimensions={0}, use_global_device_ids=true | all-gather | bytes 122880 | tf_op jit(solution)/shard_map/all_gather | solution.py:34
  132.8 90.6 %while.41 = (s32[]{:T(128)}, f32[1280,128]{1,0:T(8,128)S(1)}, f32[1280,128]{1,0:T(8,128)S(1)}, bf16[10,512,128]{2,1,0:T(8,128)(2,1)}, s32[10,512]{1,0:T(8,128)S(...) while((s32[]{:T(128)}, f32[1280,128]{1,0:T(8,128)S(1)}, ...), condition=%wide.region_10.11_spmd.clone, body=%wide.region_8.10_spmd.clone.sunk | while | flops 846560768 | bytes 16477376 | solution.py:188
  133.9 1.8 fusion.105
  135.8 1.7 convolution_add_fusion.2
  137.5 1.4 fusion.107
  138.9 1.8 fusion.108
  143.0 1.8 fusion.105
  144.8 1.7 convolution_add_fusion.2
  146.5 1.4 fusion.107
  148.0 1.8 fusion.108
  152.0 1.8 fusion.105
  153.9 1.7 convolution_add_fusion.2
  157.0 1.8 fusion.108
  161.1 1.8 fusion.105
  162.9 1.7 convolution_add_fusion.2
  164.6 1.4 fusion.107
  166.1 1.8 fusion.108
  170.2 1.8 fusion.105
  172.0 1.7 convolution_add_fusion.2
  173.7 1.4 fusion.107
  175.1 1.8 fusion.108
  179.2 1.8 fusion.105
  181.1 1.7 convolution_add_fusion.2
  184.2 1.8 fusion.108
  188.3 1.8 fusion.105
  190.1 1.7 convolution_add_fusion.2
  191.8 1.4 fusion.107
  193.2 1.8 fusion.108
  197.3 1.8 fusion.105
  199.2 1.7 convolution_add_fusion.2
  202.3 1.8 fusion.108
  206.4 1.8 fusion.105
  208.2 1.7 convolution_add_fusion.2
  211.4 1.8 fusion.108
  215.4 1.8 fusion.105
  217.3 1.7 convolution_add_fusion.2
  219.0 1.4 fusion.107
  220.4 1.8 fusion.108
  223.5 14.4 %all_to_all.15 = bf16[8,160,256]{2,1,0:T(8,128)(2,1)S(1)} all-to-all(bf16[8,160,256]{2,1,0:T(8,128)(2,1)S(1)} %bitcast.249), channel_id=1, replica_groups=mesh['row'=8,'col_0'=4,'col_1'=4,'col_2'=2] {'row'}, dimensions={0} | all-to-all | bytes 1310720 | tf_op jit(solution)/shard_map/all_to_all | solution.py:60
  237.9 7.7 %all-to-all-start = ((bf16[32,160,128]{2,1,0:T(8,128)(2,1)}), bf16[32,160,128]{2,1,0:T(8,128)(2,1)S(1)}, u32[]{:S(2)}, u32[]{:S(2)}) async-start(bf16[32,160,128]{2,1,0:T(8,128)(2,1)} %bitcast.250), calls=%async_computation | async-start | bytes 2621440 | tf_op jit(solution)/shard_map/all_to_all | solution.py:60
  245.8 34.1 %all-to-all-done = bf16[32,160,128]{2,1,0:T(8,128)(2,1)S(1)} async-done(((bf16[32,160,128]{2,1,0:T(8,128)(2,1)}), bf16[32,160,128]{2,1,0:T(8,128)(2,1)S(1)}, u32[]{:S(2)}, u32[]{:S(2)}) %all-to-all-start) | async-done | bytes 1310752 | tf_op jit(solution)/shard_map/all_to_all | solution.py:60
  280.9 2.4 copy.15
  283.4 86.1 %reduce-scatter.4.cloned.1.call-done = bf16[96,384]{1,0:T(8,128)(2,1)} async-done(((bf16[3072,384]{1,0:T(8,128)(2,1)}), bf16[96,384]{1,0:T(8,128)(2,1)}) %reduce-scatter.4.cloned.1.call-update) | async-done | bytes 73744 | tf_op jit(solution)/shard_map/reduce_scatter | solution.py:209
  369.6 1.7 broadcast_in_dim.95
  371.3 4.0 %all-to-all-start.2 = ((bf16[8,96,384]{2,1,0:T(8,128)(2,1)}), bf16[8,96,384]{2,1,0:T(8,128)(2,1)S(1)}, u32[]{:S(2)}, u32[]{:S(2)}) async-start(bf16[8,96,384]{2,1,0:T(8,128)(2,1)} %broadcast_in_dim.95), calls=%async_computation.2 | async-start | bytes 1179648 | tf_op jit(solution)/shard_map/all_to_all | solution.py:75
  375.9 7.3 %all-to-all-done.2 = bf16[8,96,384]{2,1,0:T(8,128)(2,1)S(1)} async-done(((bf16[8,96,384]{2,1,0:T(8,128)(2,1)}), bf16[8,96,384]{2,1,0:T(8,128)(2,1)S(1)}, u32[]{:S(2)}, u32[]{:S(2)}) %all-to-all-start.2) | async-done | bytes 589856 | tf_op jit(solution)/shard_map/all_to_all | solution.py:75
  (170 shorter events, 46.6 us)
Async XLA Ops:
  7.2 272.9 %copy-start = (bf16[160,3072]{1,0:T(8,128)(2,1)S(1)}, bf16[160,3072]{1,0:T(8,128)(2,1)}, u32[]{:S(2)}) copy-start(bf16[160,3072]{1,0:T(8,128)(2,1)} %param.14) | copy-start | bytes 2949124
  7.2 33.1 %copy-start.2 = (s32[320]{0:T(512)S(1)}, s32[320]{0:T(512)}, u32[]{:S(2)}) copy-start(s32[320]{0:T(512)} %param.21) | copy-start | bytes 3844
  7.2 67.3 %all-gather.8.cloned.1.call-start = ((), (), s32[]{:S(2)}) async-start(), calls=%async_computation.4 | async-start | bytes 4055040 | tf_op jit(solution)/shard_map/all_gather | solution.py:19
  237.9 42.0 %all-to-all-start = ((bf16[32,160,128]{2,1,0:T(8,128)(2,1)}), bf16[32,160,128]{2,1,0:T(8,128)(2,1)S(1)}, u32[]{:S(2)}, u32[]{:S(2)}) async-start(bf16[32,160,128]{2,1,0:T(8,128)(2,1)} %bitcast.250), calls=%async_computation | async-start | bytes 2621440 | tf_op jit(solution)/shard_map/all_to_all | solution.py:60
  245.7 123.9 %reduce-scatter.4.cloned.1.call-start = ((), (), s32[]{:S(2)}) async-start(), calls=%async_computation.5 | async-start | bytes 2433024 | tf_op jit(solution)/shard_map/reduce_scatter | solution.py:209
  280.1 0.8 copy-start.1
  371.3 11.9 %all-to-all-start.2 = ((bf16[8,96,384]{2,1,0:T(8,128)(2,1)}), bf16[8,96,384]{2,1,0:T(8,128)(2,1)S(1)}, u32[]{:S(2)}, u32[]{:S(2)}) async-start(bf16[8,96,384]{2,1,0:T(8,128)(2,1)} %broadcast_in_dim.95), calls=%async_computation.2 | async-start | bytes 1179648 | tf_op jit(solution)/shard_map/all_to_all | solution.py:75
Sparse Core Ops, SparseCore 0:
  11.1 63.3 all-gather.7
  283.5 85.9 reduce-scatter.3
where the time goes:
time: 394 us; the launch traced here: 391 us
  waiting for transfers between devices  159 us (40%)
  matrix products  95.2 us (24%)
  blocking collectives  71.1 us (18%)
  other arithmetic  24.7 us (6%)
  between operations  14.3 us (4%)
  local copies, waits for them, and re-layouts  13.4 us (3%)
  starting transfers between devices  11.8 us (3%)
    reduce_scatter x1, waiting for transfers between devices, local(): lax.psum_scatter(weight_term(layer_input, all_grads).astype(jnp.bfloat16)...  86.1 us
    all_to_all x1, waiting for transfers between devices, sum_at_owner(): lax.all_to_all(blocks, axis, split_axis=0, concat_axis=0, tiled=True)  34.1 us
    dot_general x20, matrix products, masked_scores(): lax.dot_general(query_block, key_rows, (((1,), (1,)), ((), ())), preferre...  33.9 us
    all_gather x1, waiting for transfers between devices, in_one_piece(): lax.all_gather(both, axis, axis=dim, tiled=True)  31.4 us
    all_gather x3, blocking collectives, all_in_one(): both, at, found = (lax.all_gather(jnp.concatenate(lines), axis), 0, {})  29 us
    all_gather x1, blocking collectives, in_one_piece(): lax.all_gather(both, axis, axis=dim, tiled=True)  27.6 us
    dot_general x10, matrix products, backward_block(): lax.dot_general(score_grad, query_block, (((0,), (0,)), ((), ())), prefer...  17.6 us
    dot_general x10, matrix products, backward_block(): lax.dot_general(prob_low, grad_block, (((0,), (0,)), ((), ())), preferred...  17.1 us
  transfers between devices with their start and end apart: 4, of which 4 were waited for; matrix products, arithmetic and copies ran while one was open for 2% of the time, Pallas kernels for 0%

commit v1 on v0

v1 whole, which is shorter than its diff:
```python
import math

import jax
import jax.numpy as jnp
from jax import lax
from jax.experimental import pallas as pl
from jax.experimental.pallas import tpu as pltpu
from jax.sharding import Mesh
from jax.sharding import PartitionSpec as P

BLK = 128
BIG = 16384.0
MESH = pl.DeviceIdType.MESH
NT = (((1,), (1,)), ((), ()))
AXES = ("x", "zl", "zh", "y", "c")
bf16 = jnp.bfloat16
f32 = jnp.float32


def dot_nt(a, b, **kw):
    return lax.dot_general(a, b, NT, preferred_element_type=f32, **kw)


def dot(a, b):
    return jnp.dot(a, b, preferred_element_type=f32)


def as_column(row):
    return jnp.transpose(jnp.broadcast_to(row, (128, row.shape[1])))


def eye(n):
    return (
        lax.broadcasted_iota(jnp.int32, (n, n), 0) == lax.broadcasted_iota(jnp.int32, (n, n), 1)
    ).astype(bf16)


class Group:
    def __init__(self, size, me, device_of, send, recv):
        self.size, self.me, self.device_of, self.send, self.recv = size, me, device_of, send, recv

    def copy(self, k, member, src, dst):
        return pltpu.make_async_remote_copy(
            src_ref=src,
            dst_ref=dst,
            send_sem=self.send.at[k, member],
            recv_sem=self.recv.at[k, self.me],
            device_id=self.device_of(member),
            device_id_type=MESH,
        )

    def landed(self, k, member, src, dst):
        return pltpu.make_async_remote_copy(
            src_ref=src,
            dst_ref=dst,
            send_sem=self.send.at[k, member],
            recv_sem=self.recv.at[k, member],
            device_id=self.device_of(member),
            device_id_type=MESH,
        )

    def others(self, body):
        def step(i, carry):
            body(lax.rem(self.me + i, self.size))
            return carry

        lax.fori_loop(1, self.size, step, 0)


def kernel(
    dims, q_in, k_in, v_in, o_in, g_in, x_in, pos_ref, span_ref,
    dq_out, dk_out, dv_out, wg_out,
    qb, gb, db, kb, vb, fq, fk, kt, et, ut, s_scr, dqt, st, rr, gs, qs,
    dqs, dqr, kvs, kvr, xt, xr, gr, ws, wr, ar,
    q_send, q_recv, k_send, k_recv, p_send, p_recv, w_send, w_recv, a_send, a_recv, own_sem,
):
    nx, nzl, nzh, ny, nc = dims
    tok = q_in.shape[0]
    chunk = wg_out.shape[0]
    x, zl, zh, y, c = (lax.axis_index(a) for a in AXES)
    nq, nk, npc, nr = nzh * nzl * nc, nx * ny, ny * nc, nx * nzl
    me_q = (zh * nzl + zl) * nc + c
    me_k = x * ny + y
    me_p = y * nc + c
    me_r = x * nzl + zl
    n_query, n_key = nq * tok, nk * tok

    def rows_of(s):
        return pl.ds(pl.multiple_of(s * tok, tok), tok)

    def dev(ax, azl, azh, ay, ac):
        return (ax, azl, azh, ay, ac)

    def q_dev(s):
        z = s // nc
        return dev(x, z % nzl, z // nzl, y, s % nc)

    def k_dev(s):
        return dev(s // ny, zl, zh, s % ny, c)

    def p_dev(s):
        return dev(x, zl, zh, s // nc, s % nc)

    def w_dev(s):
        return dev(x, zl, s, y, c)

    def a_dev(s):
        return dev(s // nzl, s % nzl, zh, y, c)

    gq = Group(nq, me_q, q_dev, q_send, q_recv)
    gk = Group(nk, me_k, k_dev, k_send, k_recv)
    gp = Group(npc, me_p, p_dev, p_send, p_recv)
    gw = Group(nzh, zh, w_dev, w_send, w_recv)
    ga = Group(nr, me_r, a_dev, a_send, a_recv)

    barrier = pltpu.get_barrier_semaphore()
    for group in (gq, gk, gp, gw, ga):
        group.others(
            lambda s, group=group: pl.semaphore_signal(
                barrier, inc=1, device_id=group.device_of(s), device_id_type=MESH
            )
        )

    qb[rows_of(me_q), :] = q_in[...]
    gb[rows_of(me_q), :] = g_in[...]
    kb[rows_of(me_k), :] = k_in[...]
    vb[rows_of(me_k), :] = v_in[...]
    product = g_in[...].astype(f32) * o_in[...].astype(f32)
    delta = dot_nt(jnp.ones((8, product.shape[1]), f32), product, precision=lax.Precision.HIGHEST)
    db[me_q, :, 0:tok] = delta[0:1, :]
    pl.semaphore_wait(barrier, nq + nk + npc + nzh + nr - 5)

    def start_q(s):
        gq.copy(0, s, qb.at[rows_of(me_q), :], qb.at[rows_of(me_q), :]).start()
        gq.copy(1, s, gb.at[rows_of(me_q), :], gb.at[rows_of(me_q), :]).start()
        gq.copy(2, s, db.at[me_q], db.at[me_q]).start()

    def start_k(s):
        gk.copy(0, s, kb.at[rows_of(me_k), :], kb.at[rows_of(me_k), :]).start()
        gk.copy(1, s, vb.at[rows_of(me_k), :], vb.at[rows_of(me_k), :]).start()

    gk.others(start_k)
    gq.others(start_q)

    low, high = span_ref[0:1, :], span_ref[1:2, :]
    last = lax.broadcasted_iota(jnp.int32, (tok, 128), 1) == 127

    def one_hot(device, hit, always):
        index = device[0]
        for n, i in zip(dims[1:], device[1:]):
            index = index * n + i
        col = as_column(pos_ref[pl.ds(index, 1), :])[0:tok, :]
        inside = jnp.where((col >= low) & (col < high), hit, 0.0)
        return jnp.where(last, always, inside).astype(bf16)

    def query_hot(s, carry):
        fq[pl.ds(pl.multiple_of(s * tok, tok), tok), :] = one_hot(q_dev(s), BIG, -BIG)
        return carry

    def key_hot(s, carry):
        fk[pl.ds(pl.multiple_of(s * tok, tok), tok), :] = one_hot(k_dev(s), 1.0, 1.0)
        return carry

    lax.fori_loop(0, nq, query_hot, 0)
    lax.fori_loop(0, nk, key_hot, 0)

    xt[:, :, :, tok:] = jnp.zeros((npc, nzh, chunk, 256 - tok), bf16)
    gr[:, tok:, :] = jnp.zeros((npc, 256 - tok, 384), bf16)
    four = eye(4 * chunk)
    for g in range(nzh * npc // 4):
        turned = dot_nt(four, x_in[:, g * 4 * chunk : (g + 1) * 4 * chunk]).astype(bf16)
        for j in range(4):
            n = 4 * g + j
            xt[n % npc, n // npc, :, 0:tok] = turned[j * chunk : (j + 1) * chunk, :]

    def landed_k(s):
        gk.landed(0, s, kb.at[rows_of(me_k), :], kb.at[rows_of(s), :]).wait_recv()
        gk.landed(1, s, vb.at[rows_of(me_k), :], vb.at[rows_of(s), :]).wait_recv()

    def landed_q(s):
        gq.landed(0, s, qb.at[rows_of(me_q), :], qb.at[rows_of(s), :]).wait_recv()
        gq.landed(1, s, gb.at[rows_of(me_q), :], gb.at[rows_of(s), :]).wait_recv()
        gq.landed(2, s, db.at[me_q], db.at[s]).wait_recv()

    gk.others(landed_k)
    gq.others(landed_q)

    own = pltpu.make_async_copy(xt.at[me_p], xr.at[me_p], own_sem)
    own.start()
    gp.others(lambda s: gp.copy(0, s, xt.at[s], xr.at[me_p]).start())

    tq = 256
    tk = 256 if n_key % 256 == 0 else tok
    score_scale = 1.0 / math.sqrt(128.0)
    rate = score_scale / math.log(2.0)
    unit = eye(128)
    kt[...] = dot_nt(unit, kb[...]).astype(bf16)
    rr[2:3, :] = jnp.concatenate([db[s, :, 0:tok] for s in range(nq)], axis=1)

    @pl.loop(0, n_query // tq)
    def _(t):
        at = pl.ds(pl.multiple_of(t * tq, tq), tq)
        query_tile = jnp.concatenate([qb[at, :], fq[at, :]], axis=1)
        grad_tile = gb[at, :]
        top = jnp.full((8, tq), -3.0e38, f32)
        for n in range(n_key // tk):
            span = slice(n * tk, (n + 1) * tk)
            s = dot_nt(jnp.concatenate([kb[span, :], fk[span, :]], axis=1), query_tile)
            s_scr[span, :] = s
            top = jnp.maximum(top, jnp.max(s.reshape(tk // 8, 8, tq), axis=0))
        peak = jnp.max(top, axis=0, keepdims=True)
        delta_row = rr[2:3, at]
        total = jnp.zeros((8, tq), f32)
        acc = jnp.zeros((128, tq), f32)
        for n in range(n_key // tk):
            span = slice(n * tk, (n + 1) * tk)
            e = jnp.exp2((s_scr[span, :] - peak) * rate)
            total = total + jnp.sum(e.reshape(tk // 8, 8, tq), axis=0)
            u = (e * (dot_nt(vb[span, :], grad_tile) - delta_row)).astype(bf16)
            et[span, at] = e.astype(bf16)
            ut[span, at] = u
            acc = acc + dot(kt[:, span], u)
        dqt[:, at] = acc
        rr[0:1, at] = peak
        rr[1:2, at] = jnp.sum(total, axis=0, keepdims=True)

    st[me_q] = rr[0:2, :]
    gq.others(lambda s: gq.copy(3, s, st.at[me_q], st.at[me_q]).start())
    gq.others(lambda s: gq.landed(3, s, st.at[me_q], st.at[s]).wait_recv())

    peak = st[0, 0:1, :]
    for s in range(1, nq):
        peak = jnp.maximum(peak, st[s, 0:1, :])
    total = jnp.zeros_like(peak)
    for s in range(nq):
        total = total + st[s, 1:2, :] * jnp.exp2((st[s, 0:1, :] - peak) * rate)
    rr[3:4, :] = jnp.exp2((rr[0:1, :] - peak) * rate) / total

    @pl.loop(0, n_query // tq)
    def _(t):
        at = pl.ds(pl.multiple_of(t * tq, tq), tq)
        factor = rr[3:4, at]
        dqs[at, :] = jnp.transpose(dqt[:, at] * (factor * score_scale)).astype(bf16)
        col = as_column(factor)
        gs[at, :] = (gb[at, :].astype(f32) * col).astype(bf16)
        qs[at, :] = (qb[at, :].astype(f32) * (col * score_scale)).astype(bf16)

    gq.others(lambda s: gq.copy(4, s, dqs.at[rows_of(s), :], dqr.at[me_q]).start())
    dqr[me_q] = dqs[rows_of(me_q), :]

    tb = 4 * tok if n_key % (4 * tok) == 0 else tok

    @pl.loop(0, n_key // tb)
    def _(t):
        at = pl.ds(pl.multiple_of(t * tb, tb), tb)
        kvs[at, 0:128] = dot(ut[at, :], qs[...]).astype(bf16)
        kvs[at, 128:256] = dot(et[at, :], gs[...]).astype(bf16)

    gk.others(lambda s: gk.copy(2, s, kvs.at[rows_of(s), :], kvr.at[me_k]).start())
    kvr[me_k] = kvs[rows_of(me_k), :]

    gq.others(lambda s: gq.landed(4, s, dqs.at[rows_of(s), :], dqr.at[s]).wait_recv())
    acc = dqr[0].astype(f32)
    for s in range(1, nq):
        acc = acc + dqr[s].astype(f32)
    dq_out[...] = acc.astype(bf16)
    gr[me_p, 0:tok, 0:128] = acc.astype(bf16)

    def part(n, a, b, s):
        return gp.copy(n, s, gr.at[me_p, 0:tok, a:b], gr.at[me_p, 0:tok, a:b])

    def part_landed(n, a, b, s):
        gp.landed(n, s, gr.at[me_p, 0:tok, a:b], gr.at[s, 0:tok, a:b]).wait_recv()

    gp.others(lambda s: part(1, 0, 128, s).start())

    gk.others(lambda s: gk.landed(2, s, kvs.at[rows_of(s), :], kvr.at[s]).wait_recv())
    acc = kvr[0].astype(f32)
    for s in range(1, nk):
        acc = acc + kvr[s].astype(f32)
    dk_out[...] = acc[:, 0:128].astype(bf16)
    dv_out[...] = acc[:, 128:256].astype(bf16)
    gr[me_p, 0:tok, 128:384] = acc.astype(bf16)
    gp.others(lambda s: part(2, 128, 384, s).start())

    own.wait()
    gp.others(lambda s: gp.landed(0, s, xt.at[s], xr.at[s]).wait_recv())
    gp.others(lambda s: part_landed(1, 0, 128, s))
    gp.others(lambda s: part_landed(2, 128, 384, s))

    def weight_rows(n):
        acc = dot(xr[0, n], gr[0])
        for p in range(1, npc):
            acc = acc + dot(xr[p, n], gr[p])
        return acc.astype(bf16)

    def weight_step(i, carry):
        n = lax.rem(zh + i, nzh)
        ws[n] = weight_rows(n)
        gw.copy(0, n, ws.at[n], wr.at[zh]).start()
        return carry

    lax.fori_loop(1, nzh, weight_step, 0)
    wr[zh] = weight_rows(zh)
    gw.others(lambda s: gw.landed(0, s, ws.at[s], wr.at[s]).wait_recv())
    acc = wr[0].astype(f32)
    for s in range(1, nzh):
        acc = acc + wr[s].astype(f32)
    ar[me_r] = acc.astype(bf16)
    ga.others(lambda s: ga.copy(0, s, ar.at[me_r], ar.at[me_r]).start())
    ga.others(lambda s: ga.landed(0, s, ar.at[me_r], ar.at[s]).wait_recv())
    acc = ar[0].astype(f32)
    for s in range(1, nr):
        acc = acc + ar[s].astype(f32)
    wg_out[...] = acc

    def sent_q(s):
        gq.copy(0, s, qb.at[rows_of(me_q), :], qb.at[rows_of(me_q), :]).wait_send()
        gq.copy(1, s, gb.at[rows_of(me_q), :], gb.at[rows_of(me_q), :]).wait_send()
        gq.copy(2, s, db.at[me_q], db.at[me_q]).wait_send()
        gq.copy(3, s, st.at[me_q], st.at[me_q]).wait_send()
        gq.copy(4, s, dqs.at[rows_of(s), :], dqr.at[me_q]).wait_send()

    def sent_k(s):
        gk.copy(0, s, kb.at[rows_of(me_k), :], kb.at[rows_of(me_k), :]).wait_send()
        gk.copy(1, s, vb.at[rows_of(me_k), :], vb.at[rows_of(me_k), :]).wait_send()
        gk.copy(2, s, kvs.at[rows_of(s), :], kvr.at[me_k]).wait_send()

    def sent_p(s):
        gp.copy(0, s, xt.at[s], xr.at[me_p]).wait_send()
        part(1, 0, 128, s).wait_send()
        part(2, 128, 384, s).wait_send()

    gq.others(sent_q)
    gk.others(sent_k)
    gp.others(sent_p)
    gw.others(lambda s: gw.copy(0, s, ws.at[s], wr.at[zh]).wait_send())
    ga.others(lambda s: ga.copy(0, s, ar.at[me_r], ar.at[me_r]).wait_send())


def local(
    dims, layer_input, queries, key_states, value_states, forward_out, out_grad, token_pos,
    block_sample,
):
    nx, nzl, nzh, ny, nc = dims
    tok, width = queries.shape
    depth = layer_input.shape[1]
    chunk = depth // (nzh * ny * nc)
    nq, nk, npc, nr = nzh * nzl * nc, nx * ny, ny * nc, nx * nzl
    n_query, n_key = nq * tok, nk * tok
    pos = token_pos.astype(f32).reshape(-1, tok)
    pos = jnp.pad(pos, ((0, 0), (0, 256 - tok)))
    ids = jnp.arange(128, dtype=jnp.int32)
    low = BLK * jnp.sum(block_sample[None, :] < ids[:, None], axis=1)
    high = BLK * jnp.sum(block_sample[None, :] <= ids[:, None], axis=1)
    span = jnp.stack([low, high]).astype(f32)
    span = jnp.pad(span, ((0, 6), (0, 0)))
    V = pltpu.VMEM
    dma = pltpu.SemaphoreType.DMA
    scratch = [
        V((n_query, 128), bf16), V((n_query, 128), bf16), V((nq, 1, 256), f32),
        V((n_key, 128), bf16), V((n_key, 128), bf16),
        V((n_query, 128), bf16), V((n_key, 128), bf16), V((128, n_key), bf16),
        V((n_key, n_query), bf16), V((n_key, n_query), bf16), V((n_key, 256), f32),
        V((128, n_query), f32), V((nq, 2, n_query), f32), V((8, n_query), f32),
        V((n_query, 128), bf16), V((n_query, 128), bf16),
        V((n_query, 128), bf16), V((nq, tok, 128), bf16),
        V((n_key, 256), bf16), V((nk, tok, 256), bf16),
        V((npc, nzh, chunk, 256), bf16), V((npc, nzh, chunk, 256), bf16),
        V((npc, 256, 384), bf16), V((nzh, chunk, 384), bf16), V((nzh, chunk, 384), bf16),
        V((nr, chunk, 384), bf16),
        dma((5, nq)), dma((5, nq)), dma((3, nk)), dma((3, nk)), dma((3, npc)), dma((3, npc)),
        dma((1, nzh)), dma((1, nzh)), dma((1, nr)), dma((1, nr)), dma,
    ]

    def body(*refs):
        kernel(dims, *refs)

    vmem = pl.BlockSpec(memory_space=pltpu.VMEM)
    grad = jax.ShapeDtypeStruct((tok, 128), bf16)
    return pl.pallas_call(
        body,
        out_shape=(grad, grad, grad, jax.ShapeDtypeStruct((chunk, 384), f32)),
        in_specs=[vmem] * 8,
        out_specs=(vmem,) * 4,
        scratch_shapes=scratch,
        compiler_params=pltpu.CompilerParams(
            collective_id=0, has_side_effects=True, vmem_limit_bytes=64 * 2**20
        ),
        name="packed_backward",
    )(queries, key_states, value_states, forward_out, out_grad, layer_input, pos, span)


def on_mesh(finer):
    dims = tuple(finer.shape[a] for a in AXES)
    slots, cols = P(AXES, None), P(("zh", "y", "c"), None)
    return jax.shard_map(
        lambda *args: local(dims, *args),
        mesh=finer,
        in_specs=(slots,) * 6 + (P(), P()),
        out_specs=(slots, slots, slots, cols),
        check_vma=False,
    )


def solution(mesh):
    return on_mesh(Mesh(mesh.devices.reshape(4, 2, 4, 4, 2), AXES))
```

time: 394 us -> 148 us (0.38)
  waiting for transfers between devices: 159 us -> 0 us
  Pallas kernels: 0 us -> 139 us
  matrix products: 95.2 us -> 0 us
  blocking collectives: 71.1 us -> 0 us
  other arithmetic: 24.7 us -> 1.75 us
  between operations: 14.3 us -> 0.67 us
  starting transfers between devices: 11.8 us -> 0 us
  local copies, waits for them, and re-layouts: 13.4 us -> 6.33 us
    pallas_call x0 -> x1, Pallas kernels: none -> 139 us  [local(): pl.pallas_call(body, out_shape=(grad, grad, grad, jax.ShapeDtypeStruct((c...]
    dot_general x61 -> x0, matrix products: 95.2 us -> none  [the longest x20 33.9 us: masked_scores(): lax.dot_general(query_block, key_rows, (((1,), (1,)), ((), ())), preferre...]
    reduce_scatter x1 -> x0, waiting for transfers between devices: 86.1 us -> none  [local(): lax.psum_scatter(weight_term(layer_input, all_grads).astype(jnp.bfloat16)...]
    all_gather x4 -> x0, blocking collectives: 56.6 us -> none  [the longest x3 29 us: all_in_one(): both, at, found = (lax.all_gather(jnp.concatenate(lines), axis), 0, {})]
    all_to_all x2 -> x0, waiting for transfers between devices: 41.4 us -> none  [the longest x1 34.1 us: sum_at_owner(): lax.all_to_all(blocks, axis, split_axis=0, concat_axis=0, tiled=True)]
    all_gather x1 -> x0, waiting for transfers between devices: 31.4 us -> none  [in_one_piece(): lax.all_gather(both, axis, axis=dim, tiled=True)]
    reduce_sum x34 -> x1, other arithmetic: 21.5 us -> 0.8 us  [local(): low = BLK * jnp.sum(block_sample[None, :] < ids[:, None], axis=1)]
    all_to_all x1 -> x0, blocking collectives: 14.4 us -> none  [sum_at_owner(): lax.all_to_all(blocks, axis, split_axis=0, concat_axis=0, tiled=True)]
  transfers between devices with their start and end apart: 4 -> 0, of which waited for: 4 -> 0; matrix products, arithmetic and copies ran while one was open for 2% -> 0% of each run, Pallas kernels for 0% -> 0%
where the time goes in v1:
time: 148 us; the launch traced here: 147 us
  Pallas kernels  139 us (94%)
  local copies, waits for them, and re-layouts  6.33 us (4%)
  other arithmetic  1.75 us (1%)
    pallas_call x1, Pallas kernels, local(): pl.pallas_call(body, out_shape=(grad, grad, grad, jax.ShapeDtypeStruct((c...  139 us
    unnamed x6, local copies, waits for them, and re-layouts  4.89 us

profile of v1, /device:TPU:1, one launch (start us, length us, event | category | flops | bytes accessed | tf_op | source)
XLA Modules:
  0.0 147.5 jit_solution(9704444850650998536)
XLA Ops:
  0.6 0.8 convert_reduce_fusion.1
  1.5 0.6 pad.9.refs_7_
  2.1 0.9 convert_element_type.16
  3.0 0.1 reshape.30
  3.1 0.7 pad.8.refs_6_
  3.8 138.7 %packed_backward.1 = (bf16[160,128]{1,0:T(8,128)(2,1)}, bf16[160,128]{1,0:T(8,128)(2,1)}, bf16[160,128]{1,0:T(8,128)(2,1)}, f32[96,384]{1,0:T(8,128)}) custom-call(bf16[160,128]{1,0:T(8,128)(2,1)} %refs_0_.1, bf16[160,128]{1,0:T(8,128)(2,1)} %refs_1_.1, bf16[160,128]{1,0:T(8,128)(2,1)} %refs_2_.1, bf16[160,128]{1,0:T(8,128)(2,1)} %refs_3_.1, ...), custom_call_target="tpu_custom_call" | custom-call | tf_op jit(solution)/shard_map/packed_backward/pallas_call | solution.py:381
  142.6 0.0 copy-start
  142.6 1.4 copy.16
  144.0 1.4 copy.17
  145.4 1.4 copy.18
  146.8 0.0 copy-done
  146.8 0.7 copy.19
  (2 shorter events, 0.0 us)
Async XLA Ops:
  142.6 4.2 %copy-start = (f32[96,384]{1,0:T(8,128)S(1)}, f32[96,384]{1,0:T(8,128)}, u32[]{:S(2)}) copy-start(f32[96,384]{1,0:T(8,128)} %get-tuple-element.15) | copy-start | bytes 442372

commit v2 on v1

v2 whole, which is shorter than its diff:
```python
import math

import jax
import jax.numpy as jnp
from jax import lax
from jax.experimental import pallas as pl
from jax.experimental.pallas import tpu as pltpu
from jax.sharding import Mesh
from jax.sharding import PartitionSpec as P

BLK = 128
BIG = 16384.0
MESH = pl.DeviceIdType.MESH
NT = (((1,), (1,)), ((), ()))
AXES = ("x", "zl", "zh", "y", "c")
bf16 = jnp.bfloat16
f32 = jnp.float32


def dot_nt(a, b, **kw):
    return lax.dot_general(a, b, NT, preferred_element_type=f32, **kw)


def dot(a, b):
    return jnp.dot(a, b, preferred_element_type=f32)


def as_column(row):
    return jnp.transpose(jnp.broadcast_to(row, (128, row.shape[1])))


def eye(n):
    return (
        lax.broadcasted_iota(jnp.int32, (n, n), 0) == lax.broadcasted_iota(jnp.int32, (n, n), 1)
    ).astype(bf16)


def as_row(col):
    return jnp.transpose(jnp.broadcast_to(col, (col.shape[0], 128)))[0:1, :]


def by_distance(n):
    return sorted(range(1, n), key=lambda d: -min(d, n - d))


def kernel(
    dims, q_in, k_in, v_in, o_in, g_in, x_in, pos_ref, block_ref,
    dq_out, dk_out, dv_out, wg_out,
    qg, db, kv, fq, fk, kt, et, ut, s_scr, dqt, st, rr, gs, qs, dk_acc, dv_acc,
    dqs, dqr, dks, dvs, dkr, dvr, xt, xr, gr, ws, wr, ar,
    q_send, q_recv, f_send, t_send, t_recv, k_send, k_recv, x_send, x_recv, p_send, h_send, p_recv,
    w_send, w_recv, a_send, a_recv, own_sem,
):
    nx, nzl, nzh, ny, nc = dims
    tok = q_in.shape[0]
    chunk = wg_out.shape[0]
    x, zl, zh, y, c = (lax.axis_index(a) for a in AXES)
    nz = nzh * nzl
    nq, nk, npc, nr = nz * nc, nx * ny, ny * nc, nx * nzl
    z = zh * nzl + zl
    me_q = z * nc + c
    me_k = x * ny + y
    me_p = y * nc + c
    me_r = x * nzl + zl
    n_query, n_key = nq * tok, nk * tok
    half = n_query // 2

    def rows_of(s):
        return pl.ds(pl.multiple_of(s * tok, tok), tok)

    def at_z(w, core):
        return (x, lax.rem(w, nzl), w // nzl, y, core)

    def at_xy(a, b):
        return (a, zl, zh, b, c)

    def at_p(s):
        return (x, zl, zh, s // nc, lax.rem(s, nc))

    def at_zh(s):
        return (x, zl, s, y, c)

    def at_r(s):
        return (s // nzl, lax.rem(s, nzl), zh, y, c)

    other = 1 - c
    partner = (x, zl, zh, y, other)

    def send(src, dst, send_sem, recv_sem, device):
        return pltpu.make_async_remote_copy(
            src_ref=src, dst_ref=dst, send_sem=send_sem, recv_sem=recv_sem,
            device_id=device, device_id_type=MESH,
        )

    def each(me, size, body):
        def step(i, carry):
            body(lax.rem(me + i, size))
            return carry

        lax.fori_loop(1, size, step, 0)

    def each_z(body):
        for d in by_distance(nz):
            body(lax.rem(z + d, nz))

    def each_y(body):
        for d in by_distance(ny):
            body(lax.rem(y + d, ny))

    def each_xy(body):
        pairs = [(a, b) for a in range(nx) for b in range(ny) if a or b]
        for a, b in sorted(pairs, key=lambda p: -min(p[0], nx - p[0]) - min(p[1], ny - p[1])):
            body(lax.rem(x + a, nx), lax.rem(y + b, ny))

    barrier = pltpu.get_barrier_semaphore()

    def hello(device):
        pl.semaphore_signal(barrier, inc=1, device_id=device, device_id_type=MESH)

    each(me_q, nq, lambda s: hello(at_z(s // nc, lax.rem(s, nc))))
    each(me_k, nk, lambda s: hello(at_xy(s // ny, lax.rem(s, ny))))
    each(me_p, npc, lambda s: hello(at_p(s)))
    each(zh, nzh, lambda s: hello(at_zh(s)))
    each(me_r, nr, lambda s: hello(at_r(s)))

    mine_q, mine_k = rows_of(me_q), rows_of(me_k)
    qg[mine_q, 0:128] = q_in[...]
    qg[mine_q, 128:256] = g_in[...]
    kv[mine_k, 0:128] = k_in[...]
    kv[mine_k, 128:256] = v_in[...]
    product = g_in[...].astype(f32) * o_in[...].astype(f32)
    delta = dot_nt(jnp.ones((8, product.shape[1]), f32), product, precision=lax.Precision.HIGHEST)
    db[me_q, :, 0:tok] = delta[0:1, :]
    pl.semaphore_wait(barrier, nq + nk + npc + nzh + nr - 5)

    def q_block(s, device, sem, n):
        rows = rows_of(s)
        return (
            send(qg.at[rows, :], qg.at[rows, :], sem.at[0, n], q_recv.at[0, s], device),
            send(db.at[s], db.at[s], sem.at[1, n], q_recv.at[1, s], device),
        )

    def k_block(s, device, n):
        rows = rows_of(s)
        return send(kv.at[rows, :], kv.at[rows, :], k_send.at[0, n], k_recv.at[0, s], device)

    def start_q(s, device, sem, n):
        for copy in q_block(s, device, sem, n):
            copy.start()

    each_z(lambda w: start_q(me_q, at_z(w, c), q_send, w))
    each_xy(lambda a, b: k_block(me_k, at_xy(a, b), a * ny + b).start())
    start_q(me_q, partner, f_send, z)

    samples = lax.broadcasted_iota(jnp.int32, (128, block_ref.shape[1]), 0)
    below = jnp.where(block_ref[...] < samples, 1.0, 0.0)
    upto = jnp.where(block_ref[...] <= samples, 1.0, 0.0)
    low = as_row(jnp.sum(below, axis=1, keepdims=True) * float(BLK))
    high = as_row(jnp.sum(upto, axis=1, keepdims=True) * float(BLK))
    last = lax.broadcasted_iota(jnp.int32, (tok, 128), 1) == 127
    rest = jnp.zeros((1, 256 - tok), f32)

    def one_hot(device, hit, always):
        index = device[0]
        for n, i in zip(dims[1:], device[1:]):
            index = index * n + i
        row = jnp.concatenate([pos_ref[pl.ds(index, 1), :].astype(f32), rest], axis=1)
        col = as_column(row)[0:tok, :]
        inside = jnp.where((col >= low) & (col < high), hit, 0.0)
        return jnp.where(last, always, inside).astype(bf16)

    def query_hot(s, carry):
        fq[rows_of(s), :] = one_hot(at_z(s // nc, lax.rem(s, nc)), BIG, -BIG)
        return carry

    def key_hot(s, carry):
        fk[rows_of(s), :] = one_hot(at_xy(s // ny, lax.rem(s, ny)), 1.0, 1.0)
        return carry

    lax.fori_loop(0, nk, key_hot, 0)

    def land_q(w):
        s = w * nc + c
        for copy in q_block(s, partner, f_send, w):
            copy.wait_recv()
        start_q(s, partner, f_send, w)

    each_z(land_q)
    lax.fori_loop(0, nq, query_hot, 0)

    xt[:, :, tok:] = jnp.zeros((npc, nzh * chunk, 256 - tok), bf16)
    gr[:, tok:, :] = jnp.zeros((npc, 256 - tok, 384), bf16)
    four = eye(4 * chunk)
    for g in range(nzh * npc // 4):
        turned = dot_nt(four, x_in[:, g * 4 * chunk : (g + 1) * 4 * chunk]).astype(bf16)
        for j in range(4):
            n = 4 * g + j
            rows = slice(n // npc * chunk, (n // npc + 1) * chunk)
            xt[n % npc, rows, 0:tok] = turned[j * chunk : (j + 1) * chunk, :]

    each_xy(lambda a, b: k_block(a * ny + b, at_xy(a, b), a * ny + b).wait_recv())

    def land_other(w, carry):
        for copy in q_block(w * nc + other, partner, f_send, w):
            copy.wait_recv()
        return carry

    lax.fori_loop(0, nz, land_other, 0)

    def x_block(s, n):
        return send(xt.at[s], xr.at[n], x_send.at[s], x_recv.at[n], at_p(s))

    own = pltpu.make_async_copy(xt.at[me_p], xr.at[me_p], own_sem)
    own.start()
    each(me_p, npc, lambda s: x_block(s, me_p).start())

    tq = 256 if half % 256 == 0 else 128
    tk = 256 if n_key % 256 == 0 else tok
    score_scale = 1.0 / math.sqrt(128.0)
    rate = score_scale / math.log(2.0)
    kt[...] = dot_nt(eye(128), kv[:, 0:128]).astype(bf16)
    rr[2:3, :] = jnp.concatenate([db[s, :, 0:tok] for s in range(nq)], axis=1)

    def score_tile(t, with_dq):
        at = pl.ds(pl.multiple_of(t * tq, tq), tq)
        query_tile = jnp.concatenate([qg[at, 0:128], fq[at, :]], axis=1)
        grad_tile = qg[at, 128:256]
        top = jnp.full((8, tq), -3.0e38, f32)
        for n in range(n_key // tk):
            span = slice(n * tk, (n + 1) * tk)
            s = dot_nt(jnp.concatenate([kv[span, 0:128], fk[span, :]], axis=1), query_tile)
            s_scr[span, 0:tq] = s
            top = jnp.maximum(top, jnp.max(s.reshape(tk // 8, 8, tq), axis=0))
        peak = jnp.max(top, axis=0, keepdims=True)
        delta_row = rr[2:3, at]
        total = jnp.zeros((8, tq), f32)
        acc = jnp.zeros((128, tq), f32)
        for n in range(n_key // tk):
            span = slice(n * tk, (n + 1) * tk)
            e = jnp.exp2((s_scr[span, 0:tq] - peak) * rate)
            total = total + jnp.sum(e.reshape(tk // 8, 8, tq), axis=0)
            u = (e * (dot_nt(kv[span, 128:256], grad_tile) - delta_row)).astype(bf16)
            et[span, at] = e.astype(bf16)
            ut[span, at] = u
            if with_dq:
                acc = acc + dot(kt[:, span], u)
        if with_dq:
            dqt[:, at] = acc
        rr[0:1, at] = peak
        rr[1:2, at] = jnp.sum(total, axis=0, keepdims=True)

    def st_block(h, s, device, n):
        return send(st.at[h, s], st.at[h, s], t_send.at[h, n], t_recv.at[h, s], device)

    def send_stats(h):
        st[h, me_q] = rr[0:2, h * half : (h + 1) * half]
        each(me_q, nq, lambda s: st_block(h, me_q, at_z(s // nc, lax.rem(s, nc)), s).start())

    def dq_block(s, n):
        device = at_z(s // nc, lax.rem(s, nc))
        return send(dqs.at[rows_of(s), :], dqr.at[n], q_send.at[2, s], q_recv.at[2, n], device)

    def factors(h):
        each(me_q, nq, lambda s: st_block(h, s, partner, s).wait_recv())
        part = slice(h * half, (h + 1) * half)
        peak = st[h, 0, 0:1, :]
        for s in range(1, nq):
            peak = jnp.maximum(peak, st[h, s, 0:1, :])
        total = jnp.zeros_like(peak)
        for s in range(nq):
            total = total + st[h, s, 1:2, :] * jnp.exp2((st[h, s, 0:1, :] - peak) * rate)
        rr[3:4, part] = jnp.exp2((rr[0:1, part] - peak) * rate) / total

        @pl.loop(h * half // tq, (h + 1) * half // tq)
        def _(t):
            at = pl.ds(pl.multiple_of(t * tq, tq), tq)
            factor = rr[3:4, at]
            dqs[at, :] = jnp.transpose(dqt[:, at] * (factor * score_scale)).astype(bf16)
            col = as_column(factor)
            gs[at, :] = (qg[at, 128:256].astype(f32) * col).astype(bf16)
            qs[at, :] = (qg[at, 0:128].astype(f32) * (col * score_scale)).astype(bf16)

        def send_dq(s, carry):
            @pl.when(s != me_q)
            def _():
                dq_block(s, me_q).start()

            return carry

        lax.fori_loop(h * nq // 2, (h + 1) * nq // 2, send_dq, 0)

    @pl.loop(0, half // tq)
    def _(t):
        score_tile(t, True)

    send_stats(0)

    @pl.loop(half // tq, n_query // tq)
    def _(t):
        score_tile(t, False)

    send_stats(1)

    @pl.loop(half // tq, n_query // tq)
    def _(t):
        at = pl.ds(pl.multiple_of(t * tq, tq), tq)
        dqt[:, at] = dot(kt[...], ut[:, at])

    factors(0)

    tb = ny * tok

    @pl.loop(0, nx)
    def _(t):
        at = pl.ds(pl.multiple_of(t * tb, tb), tb)
        dk_acc[at, :] = dot(ut[at, 0:half], qs[0:half, :])
        dv_acc[at, :] = dot(et[at, 0:half], gs[0:half, :])

    factors(1)
    dqr[me_q] = dqs[mine_q, :]

    def kv_block(j, s, n):
        src, dst = ((dks, dkr), (dvs, dvr))[j]
        device = at_xy(s // ny, lax.rem(s, ny))
        return send(src.at[rows_of(s), :], dst.at[n], k_send.at[1 + j, s], k_recv.at[1 + j, n], device)

    def grad_tiles(j):
        out, acc, left, right = ((dks, dk_acc, ut, qs), (dvs, dv_acc, et, gs))[j]

        def step(i, carry):
            t = lax.rem(x + 2 + i, nx)
            at = pl.ds(pl.multiple_of(t * tb, tb), tb)
            out[at, :] = (acc[at, :] + dot(left[at, half:], right[half:, :])).astype(bf16)
            for b in range(ny):
                s = t * ny + b

                @pl.when(s != me_k)
                def _():
                    kv_block(j, s, me_k).start()

            return carry

        lax.fori_loop(0, nx, step, 0)

    def summed(ref):
        acc = ref[0].astype(f32)
        for s in range(1, ref.shape[0]):
            acc = acc + ref[s].astype(f32)
        return acc

    def g_block(j, s, device, sem, n):
        ref = gr.at[s, 0:tok, 128 * j : 128 * j + 128]
        return send(ref, ref, sem.at[j, n], p_recv.at[j, s], device)

    def send_grad(j, ref, out):
        value = summed(ref).astype(bf16)
        out[...] = value
        gr[me_p, 0:tok, 128 * j : 128 * j + 128] = value
        each_y(lambda b: g_block(j, me_p, (x, zl, zh, b, c), p_send, b).start())
        g_block(j, me_p, partner, h_send, y).start()

    def w_block(j, s, n):
        return send(ws.at[j, s], wr.at[j, n], w_send.at[j, s], w_recv.at[j, n], at_zh(s))

    def send_weight(j):
        def land(b):
            s = b * nc + c
            g_block(j, s, partner, h_send, b).wait_recv()
            g_block(j, s, partner, h_send, b).start()

        each_y(land)

        def land_rest(b, carry):
            g_block(j, b * nc + other, partner, h_send, b).wait_recv()
            return carry

        lax.fori_loop(0, ny, land_rest, 0)
        acc = dot(xr[0], gr[0, :, 128 * j : 128 * j + 128])
        for p in range(1, npc):
            acc = acc + dot(xr[p], gr[p, :, 128 * j : 128 * j + 128])
        for n in range(nzh):
            ws[j, n] = acc[n * chunk : (n + 1) * chunk, :].astype(bf16)
        each(zh, nzh, lambda s: w_block(j, s, zh).start())
        wr[j, zh] = ws[j, zh]

    def a_block(j, s, n):
        return send(ar.at[j, n], ar.at[j, n], a_send.at[j, s], a_recv.at[j, n], at_r(s))

    def send_rows(j):
        each(zh, nzh, lambda s: w_block(j, s, s).wait_recv())
        ar[j, me_r] = summed(wr.at[j]).astype(bf16)
        each(me_r, nr, lambda s: a_block(j, s, me_r).start())

    def finish(j):
        each(me_r, nr, lambda s: a_block(j, s, s).wait_recv())
        wg_out[:, 128 * j : 128 * j + 128] = summed(ar.at[j])

    grad_tiles(0)
    dkr[me_k] = dks[mine_k, :]
    grad_tiles(1)
    dvr[me_k] = dvs[mine_k, :]
    each(me_q, nq, lambda s: dq_block(s, s).wait_recv())
    send_grad(0, dqr, dq_out)
    own.wait()
    each(me_p, npc, lambda s: x_block(s, s).wait_recv())
    each(me_k, nk, lambda s: kv_block(0, s, s).wait_recv())
    send_grad(1, dkr, dk_out)
    send_weight(0)
    each(me_k, nk, lambda s: kv_block(1, s, s).wait_recv())
    send_grad(2, dvr, dv_out)
    send_weight(1)
    send_rows(0)
    send_weight(2)
    send_rows(1)
    finish(0)
    send_rows(2)
    finish(1)
    finish(2)

    def q_left(w):
        for copy in q_block(me_q, partner, q_send, w):
            copy.wait_send()

    each_z(q_left)

    def f_left(w, carry):
        for copy in q_block(me_q, partner, f_send, w):
            copy.wait_send()
        return carry

    lax.fori_loop(0, nz, f_left, 0)

    def st_left(s):
        for h in range(2):
            st_block(h, me_q, partner, s).wait_send()
        dq_block(s, me_q).wait_send()

    each(me_q, nq, st_left)

    def k_left(s):
        k_block(me_k, partner, s).wait_send()
        for j in range(2):
            kv_block(j, s, me_k).wait_send()

    each(me_k, nk, k_left)
    each(me_p, npc, lambda s: x_block(s, me_p).wait_send())

    for j in range(3):
        each_y(lambda b: g_block(j, me_p, partner, p_send, b).wait_send())

        def h_left(b, carry):
            g_block(j, me_p, partner, h_send, b).wait_send()
            return carry

        lax.fori_loop(0, ny, h_left, 0)
        each(zh, nzh, lambda s: w_block(j, s, zh).wait_send())
        each(me_r, nr, lambda s: a_block(j, s, me_r).wait_send())


def local(
    dims, layer_input, queries, key_states, value_states, forward_out, out_grad, token_pos,
    block_sample,
):
    nx, nzl, nzh, ny, nc = dims
    tok, width = queries.shape
    depth = layer_input.shape[1]
    chunk = depth // (nzh * ny * nc)
    nq, nk, npc, nr = nzh * nzl * nc, nx * ny, ny * nc, nx * nzl
    n_query, n_key = nq * tok, nk * tok
    pos = token_pos.reshape(-1, tok)
    blocks = block_sample.reshape(1, -1)
    nz = nzh * nzl
    V = pltpu.VMEM
    dma = pltpu.SemaphoreType.DMA
    scratch = [
        V((n_query, 256), bf16), V((nq, 1, 256), f32), V((n_key, 256), bf16),
        V((n_query, 128), bf16), V((n_key, 128), bf16), V((128, n_key), bf16),
        V((n_key, n_query), bf16), V((n_key, n_query), bf16), V((n_key, 256), f32),
        V((128, n_query), f32), V((2, nq, 2, n_query // 2), f32), V((8, n_query), f32),
        V((n_query, 128), bf16), V((n_query, 128), bf16),
        V((n_key, 128), f32), V((n_key, 128), f32),
        V((n_query, 128), bf16), V((nq, tok, 128), bf16),
        V((n_key, 128), bf16), V((n_key, 128), bf16),
        V((nk, tok, 128), bf16), V((nk, tok, 128), bf16),
        V((npc, nzh * chunk, 256), bf16), V((npc, nzh * chunk, 256), bf16),
        V((npc, 256, 384), bf16), V((3, nzh, chunk, 128), bf16), V((3, nzh, chunk, 128), bf16),
        V((3, nr, chunk, 128), bf16),
        dma((3, nq)), dma((3, nq)), dma((2, nz)), dma((2, nq)), dma((2, nq)),
        dma((3, nk)), dma((3, nk)), dma((npc,)), dma((npc,)),
        dma((3, ny)), dma((3, ny)), dma((3, npc)),
        dma((3, nzh)), dma((3, nzh)), dma((3, nr)), dma((3, nr)), dma,
    ]

    def body(*refs):
        kernel(dims, *refs)

    vmem = pl.BlockSpec(memory_space=pltpu.VMEM)
    grad = jax.ShapeDtypeStruct((tok, 128), bf16)
    return pl.pallas_call(
        body,
        out_shape=(grad, grad, grad, jax.ShapeDtypeStruct((chunk, 384), f32)),
        in_specs=[vmem] * 8,
        out_specs=(vmem,) * 4,
        scratch_shapes=scratch,
        compiler_params=pltpu.CompilerParams(
            collective_id=0, has_side_effects=True, vmem_limit_bytes=64 * 2**20
        ),
        name="packed_backward",
    )(queries, key_states, value_states, forward_out, out_grad, layer_input, pos, blocks)


def on_mesh(finer):
    dims = tuple(finer.shape[a] for a in AXES)
    slots, cols = P(AXES, None), P(("zh", "y", "c"), None)
    return jax.shard_map(
        lambda *args: local(dims, *args),
        mesh=finer,
        in_specs=(slots,) * 6 + (P(), P()),
        out_specs=(slots, slots, slots, cols),
        check_vma=False,
    )


def solution(mesh):
    return on_mesh(Mesh(mesh.devices.reshape(4, 2, 4, 4, 2), AXES))
```

time: 148 us -> 109 us (0.74)
  Pallas kernels: 139 us -> 100 us
  other arithmetic: 1.75 us -> 0 us
  local copies, waits for them, and re-layouts: 6.33 us -> 7.88 us
    pallas_call x1, Pallas kernels: 139 us -> 100 us  [local(): pl.pallas_call(body, out_shape=(grad, grad, grad, jax.ShapeDtypeStruct((c...]
    reshape x1 -> x2, local copies, waits for them, and re-layouts: 0.13 us -> 2.98 us  [the longest x1 1.74 us: local(): pos = token_pos.reshape(-1, tok)]
where the time goes in v2:
time: 109 us
  Pallas kernels  100 us (92%)
  local copies, waits for them, and re-layouts  7.88 us (7%)
    pallas_call x1, Pallas kernels, local(): pl.pallas_call(body, out_shape=(grad, grad, grad, jax.ShapeDtypeStruct((c...  100 us
    unnamed x6, local copies, waits for them, and re-layouts  4.89 us

profile of v2, /device:TPU:1, one launch (start us, length us, event | category | flops | bytes accessed | tf_op | source)
XLA Modules:
  0.0 108.6 jit_solution(11603656313815908515)
XLA Ops:
  0.6 1.2 %reshape.15.refs_7_ = s32[1,320]{1,0:T(1,128)} reshape(s32[320]{0:T(512)} %param.15) | data formatting | bytes 2560 | tf_op jit(solution)/shard_map/reshape | solution.py:471
  1.9 1.7 %reshape.14.refs_6_ = s32[256,160]{1,0:T(8,128)} reshape(s32[40960]{0:T(1024)} %param.14) | data formatting | bytes 327680 | tf_op jit(solution)/shard_map/reshape | solution.py:470
  3.6 100.1 %packed_backward.1 = (bf16[160,128]{1,0:T(8,128)(2,1)}, bf16[160,128]{1,0:T(8,128)(2,1)}, bf16[160,128]{1,0:T(8,128)(2,1)}, f32[96,384]{1,0:T(8,128)}) custom-call(bf16[160,128]{1,0:T(8,128)(2,1)} %refs_0_.1, bf16[160,128]{1,0:T(8,128)(2,1)} %refs_1_.1, bf16[160,128]{1,0:T(8,128)(2,1)} %refs_2_.1, bf16[160,128]{1,0:T(8,128)(2,1)} %refs_3_.1, ...), custom_call_target="tpu_custom_call" | custom-call | tf_op jit(solution)/shard_map/packed_backward/pallas_call | solution.py:499
  103.7 0.0 copy-start
  103.7 1.4 %copy.16 = bf16[160,128]{1,0:T(8,128)(2,1)} copy(bf16[160,128]{1,0:T(8,128)(2,1)} %get-tuple-element.8) | data formatting | bytes 81920
  105.1 1.4 %copy.17 = bf16[160,128]{1,0:T(8,128)(2,1)} copy(bf16[160,128]{1,0:T(8,128)(2,1)} %get-tuple-element.9) | data formatting | bytes 81920
  106.5 1.4 %copy.18 = bf16[160,128]{1,0:T(8,128)(2,1)} copy(bf16[160,128]{1,0:T(8,128)(2,1)} %get-tuple-element.10) | data formatting | bytes 81920
  107.9 0.0 copy-done
  107.9 0.7 copy.19
Async XLA Ops:
  103.7 4.2 %copy-start = (f32[96,384]{1,0:T(8,128)S(1)}, f32[96,384]{1,0:T(8,128)}, u32[]{:S(2)}) copy-start(f32[96,384]{1,0:T(8,128)} %get-tuple-element.11) | copy-start | bytes 442372

commit v3 on v2

v3 whole, which is shorter than its diff:
```python
import math

import jax
import jax.numpy as jnp
from jax import lax
from jax.experimental import pallas as pl
from jax.experimental.pallas import tpu as pltpu
from jax.sharding import Mesh
from jax.sharding import PartitionSpec as P

BLK = 128
BIG = 16384.0
MESH = pl.DeviceIdType.MESH
NT = (((1,), (1,)), ((), ()))
AXES = ("x", "zl", "zh", "y", "c")
bf16 = jnp.bfloat16
f32 = jnp.float32


def dot_nt(a, b, **kw):
    return lax.dot_general(a, b, NT, preferred_element_type=f32, **kw)


def dot(a, b):
    return jnp.dot(a, b, preferred_element_type=f32)


def as_column(row):
    return jnp.transpose(jnp.broadcast_to(row, (128, row.shape[1])))


def eye(n):
    return (
        lax.broadcasted_iota(jnp.int32, (n, n), 0) == lax.broadcasted_iota(jnp.int32, (n, n), 1)
    ).astype(bf16)


def by_distance(n):
    return sorted(range(1, n), key=lambda d: -min(d, n - d))


def kernel(
    dims, q_in, k_in, v_in, o_in, g_in, x_in, pos_ref, block_ref,
    dq_out, dk_out, dv_out, wg_out,
    qb, gb, ob, db, kb, vb, xb, pos, blocks, column, fq, fk, kt, et, ut, s_scr, dqt, st, rr, gs, qs,
    dqs, dqp, dqc, dqr, dks, dvs, dkr, dvr, xt, xr, gr, ws, wr, ar, wg,
    q_send, q_recv, f_send, t_send, t_recv, e_send, e_recv, d_send, d_recv, k_send, k_recv,
    x_send, x_recv, p_send, h_send, p_recv, w_send, w_recv, a_send, a_recv, own_sem, in_sem, out_sem,
):
    nx, nzl, nzh, ny, nc = dims
    tok = q_in.shape[0]
    chunk = wg_out.shape[0]
    n_block = block_ref.shape[0]
    x, zl, zh, y, c = (lax.axis_index(a) for a in AXES)
    nz = nzh * nzl
    nq, nk, npc, nr = nz * nc, nx * ny, ny * nc, nx * nzl
    z = zh * nzl + zl
    me_q = z * nc + c
    me_k = x * ny + y
    me_p = y * nc + c
    me_r = x * nzl + zl
    n_query, n_key = nq * tok, nk * tok
    half = n_query // 2

    def rows_of(s):
        return pl.ds(pl.multiple_of(s * tok, tok), tok)

    def at_z(w, core):
        return (x, lax.rem(w, nzl), w // nzl, y, core)

    def at_xy(a, b):
        return (a, zl, zh, b, c)

    def at_p(s):
        return (x, zl, zh, s // nc, lax.rem(s, nc))

    def at_zh(s):
        return (x, zl, s, y, c)

    def at_r(s):
        return (s // nzl, lax.rem(s, nzl), zh, y, c)

    other = 1 - c
    partner = (x, zl, zh, y, other)

    def send(src, dst, send_sem, recv_sem, device):
        return pltpu.make_async_remote_copy(
            src_ref=src, dst_ref=dst, send_sem=send_sem, recv_sem=recv_sem,
            device_id=device, device_id_type=MESH,
        )

    def each(me, size, body):
        def step(i, carry):
            body(lax.rem(me + i, size))
            return carry

        lax.fori_loop(1, size, step, 0)

    def each_z(body):
        for d in by_distance(nz):
            body(lax.rem(z + d, nz))

    def each_y(body):
        for d in by_distance(ny):
            body(lax.rem(y + d, ny))

    def each_xy(body):
        pairs = [(a, b) for a in range(nx) for b in range(ny) if a or b]
        for a, b in sorted(pairs, key=lambda p: -min(p[0], nx - p[0]) - min(p[1], ny - p[1])):
            body(lax.rem(x + a, nx), lax.rem(y + b, ny))

    mine_q, mine_k = rows_of(me_q), rows_of(me_k)
    staged = [
        pltpu.make_async_copy(src, dst, in_sem.at[i])
        for i, (src, dst) in enumerate(
            (
                (k_in, kb.at[mine_k, :]), (q_in, qb.at[mine_q, :]), (v_in, vb.at[mine_k, :]),
                (g_in, gb.at[mine_q, :]), (o_in, ob), (pos_ref, pos), (block_ref, blocks), (x_in, xb),
            )
        )
    ]
    for copy in staged:
        copy.start()

    barrier = pltpu.get_barrier_semaphore()

    def hello(device):
        pl.semaphore_signal(barrier, inc=1, device_id=device, device_id_type=MESH)

    each(me_q, nq, lambda s: hello(at_z(s // nc, lax.rem(s, nc))))
    each(me_k, nk, lambda s: hello(at_xy(s // ny, lax.rem(s, ny))))
    each(me_p, npc, lambda s: hello(at_p(s)))
    each(zh, nzh, lambda s: hello(at_zh(s)))
    each(me_r, nr, lambda s: hello(at_r(s)))

    for copy in staged[:5]:
        copy.wait()
    product = gb[mine_q, :].astype(f32) * ob[...].astype(f32)
    delta = dot_nt(jnp.ones((8, product.shape[1]), f32), product, precision=lax.Precision.HIGHEST)
    db[me_q, :, 0:tok] = delta[0:1, :]
    pl.semaphore_wait(barrier, nq + nk + npc + nzh + nr - 5)

    def q_block(m, s, device, sem, n):
        ref = (qb.at[rows_of(s), :], gb.at[rows_of(s), :], db.at[s])[m]
        return send(ref, ref, sem.at[m, n], q_recv.at[m, s], device)

    def k_block(m, s, device, n):
        ref = (kb, vb)[m].at[rows_of(s), :]
        return send(ref, ref, k_send.at[m, n], k_recv.at[m, s], device)

    def start_q(m):
        each_z(lambda w: q_block(m, me_q, at_z(w, c), q_send, w).start())
        q_block(m, me_q, partner, f_send, z).start()

    def start_k(m):
        each_xy(lambda a, b: k_block(m, me_k, at_xy(a, b), a * ny + b).start())

    def hand_on(m):
        def land(w):
            s = w * nc + c
            q_block(m, s, partner, f_send, w).wait_recv()
            q_block(m, s, partner, f_send, w).start()

        each_z(land)

    def land_q(m):
        def land(w, carry):
            q_block(m, w * nc + other, partner, f_send, w).wait_recv()
            return carry

        lax.fori_loop(0, nz, land, 0)

    def land_k(m):
        each_xy(lambda a, b: k_block(m, a * ny + b, at_xy(a, b), a * ny + b).wait_recv())

    start_q(0)
    start_k(0)
    start_q(2)
    start_q(1)
    start_k(1)

    for copy in staged[5:]:
        copy.wait()
    samples = lax.broadcasted_iota(jnp.int32, (1, 128), 1)

    def count(b, carry):
        below, upto = carry
        sample = blocks[b]
        return (
            below + jnp.where(sample < samples, float(BLK), 0.0),
            upto + jnp.where(sample <= samples, float(BLK), 0.0),
        )

    none = jnp.zeros((1, 128), f32)
    low, high = lax.fori_loop(0, n_block, count, (none, none))
    last = lax.broadcasted_iota(jnp.int32, (tok, 128), 1) == 127

    def one_hot(device, hit, always):
        index = device[0]
        for n, i in zip(dims[1:], device[1:]):
            index = index * n + i
        first = index * tok // 128
        skip = pl.multiple_of(lax.rem(index * tok, 128), 32)
        row = jnp.concatenate([pos[pl.ds(first, 1), :], pos[pl.ds(first + 1, 1), :]], axis=1)
        column[...] = as_column(row.astype(f32))
        col = column[pl.ds(skip, tok), :]
        inside = jnp.where((col >= low) & (col < high), hit, 0.0)
        return jnp.where(last, always, inside).astype(bf16)

    def query_hot(s, carry):
        fq[rows_of(s), :] = one_hot(at_z(s // nc, lax.rem(s, nc)), BIG, -BIG)
        return carry

    def key_hot(s, carry):
        fk[rows_of(s), :] = one_hot(at_xy(s // ny, lax.rem(s, ny)), 1.0, 1.0)
        return carry

    lax.fori_loop(0, nk, key_hot, 0)

    hand_on(0)
    lax.fori_loop(0, nq, query_hot, 0)

    xt[:, :, tok:] = jnp.zeros((npc, nzh * chunk, 256 - tok), bf16)
    gr[:, tok:, :] = jnp.zeros((npc, 256 - tok, 384), bf16)
    four = eye(4 * chunk)
    for g in range(nzh * npc // 4):
        turned = dot_nt(four, xb[:, g * 4 * chunk : (g + 1) * 4 * chunk]).astype(bf16)
        for j in range(4):
            n = 4 * g + j
            rows = slice(n // npc * chunk, (n // npc + 1) * chunk)
            xt[n % npc, rows, 0:tok] = turned[j * chunk : (j + 1) * chunk, :]

    land_k(0)
    land_q(0)

    def x_block(s, n):
        return send(xt.at[s], xr.at[n], x_send.at[s], x_recv.at[n], at_p(s))

    own = pltpu.make_async_copy(xt.at[me_p], xr.at[me_p], own_sem)
    own.start()
    each(me_p, npc, lambda s: x_block(s, me_p).start())

    tq = 256 if half % 256 == 0 else 128
    tk = 256 if n_key % 256 == 0 else tok
    score_scale = 1.0 / math.sqrt(128.0)
    rate = score_scale / math.log(2.0)
    kt[...] = dot_nt(eye(128), kb[...]).astype(bf16)

    def tile(t):
        return pl.ds(pl.multiple_of(t * tq, tq), tq)

    def score_tile(t):
        at = tile(t)
        query_tile = jnp.concatenate([qb[at, :], fq[at, :]], axis=1)
        top = jnp.full((8, tq), -3.0e38, f32)
        for n in range(n_key // tk):
            span = slice(n * tk, (n + 1) * tk)
            s = dot_nt(jnp.concatenate([kb[span, :], fk[span, :]], axis=1), query_tile)
            s_scr[span, 0:tq] = s
            top = jnp.maximum(top, jnp.max(s.reshape(tk // 8, 8, tq), axis=0))
        peak = jnp.max(top, axis=0, keepdims=True)
        total = jnp.zeros((8, tq), f32)
        for n in range(n_key // tk):
            span = slice(n * tk, (n + 1) * tk)
            e = jnp.exp2((s_scr[span, 0:tq] - peak) * rate)
            total = total + jnp.sum(e.reshape(tk // 8, 8, tq), axis=0)
            et[span, at] = e.astype(bf16)
        rr[0:1, at] = peak
        rr[1:2, at] = jnp.sum(total, axis=0, keepdims=True)

    def grad_tile(t):
        at = tile(t)
        grad_rows = gb[at, :]
        delta_row = rr[2:3, at]
        acc = jnp.zeros((128, tq), f32)
        for n in range(n_key // tk):
            span = slice(n * tk, (n + 1) * tk)
            slope = dot_nt(vb[span, :], grad_rows) - delta_row
            u = (et[span, at].astype(f32) * slope).astype(bf16)
            ut[span, at] = u
            acc = acc + dot(kt[:, span], u)
        dqt[:, at] = acc

    def st_block(h, s, device, n):
        return send(st.at[h, s], st.at[h, s], t_send.at[h, n], t_recv.at[h, s], device)

    def send_stats(h):
        st[h, me_q] = rr[0:2, h * half : (h + 1) * half]
        each(me_q, nq, lambda s: st_block(h, me_q, at_z(s // nc, lax.rem(s, nc)), s).start())

    def factors(h):
        each(me_q, nq, lambda s: st_block(h, s, partner, s).wait_recv())
        part = slice(h * half, (h + 1) * half)
        peak = st[h, 0, 0:1, :]
        for s in range(1, nq):
            peak = jnp.maximum(peak, st[h, s, 0:1, :])
        total = jnp.zeros_like(peak)
        for s in range(nq):
            total = total + st[h, s, 1:2, :] * jnp.exp2((st[h, s, 0:1, :] - peak) * rate)
        rr[3:4, part] = jnp.exp2((rr[0:1, part] - peak) * rate) / total

    def scale_rows(t):
        at = tile(t)
        factor = rr[3:4, at]
        dqs[at, :] = jnp.transpose(dqt[:, at] * (factor * score_scale)).astype(bf16)
        col = as_column(factor)
        gs[at, :] = (gb[at, :].astype(f32) * col).astype(bf16)
        qs[at, :] = (qb[at, :].astype(f32) * (col * score_scale)).astype(bf16)

    tiles = n_query // tq
    most = tiles - max(1, tiles // 5)
    pl.loop(0, tiles // 2)(score_tile)
    send_stats(0)
    pl.loop(tiles // 2, most)(score_tile)
    hand_on(2)
    hand_on(1)
    pl.loop(most, tiles)(score_tile)
    send_stats(1)
    land_k(1)
    land_q(2)
    land_q(1)
    rr[2:3, :] = jnp.concatenate([db[s, :, 0:tok] for s in range(nq)], axis=1)
    pl.loop(0, tiles)(grad_tile)
    factors(0)
    factors(1)
    pl.loop(0, tiles)(scale_rows)

    def pair_block(w, core):
        src = dqs.at[rows_of(w * nc + core), :]
        return send(src, dqp.at[w], e_send.at[w], e_recv.at[w], partner)

    def dq_block(w, n):
        return send(dqc.at[w], dqr.at[n], d_send.at[w], d_recv.at[n], at_z(w, c))

    def send_pair(w, carry):
        pair_block(w, other).start()
        return carry

    lax.fori_loop(0, nz, send_pair, 0)

    def send_dq():
        def add(w):
            pair_block(w, c).wait_recv()
            mine = dqs[rows_of(w * nc + c), :].astype(f32)
            dqc[w] = (mine + dqp[w].astype(f32)).astype(bf16)

        def step(w):
            add(w)
            dq_block(w, z).start()

        each_z(step)
        add(z)
        dqr[z] = dqc[z]

    tb = ny * tok

    def kv_block(j, s, n):
        src, dst = ((dks, dkr), (dvs, dvr))[j]
        device = at_xy(s // ny, lax.rem(s, ny))
        return send(src.at[rows_of(s), :], dst.at[n], k_send.at[2 + j, s], k_recv.at[2 + j, n], device)

    def grad_tiles(j, first, end):
        out, left, right = ((dks, ut, qs), (dvs, et, gs))[j]

        def step(i, carry):
            t = lax.rem(x + 2 + i, nx)
            at = pl.ds(pl.multiple_of(t * tb, tb), tb)
            out[at, :] = dot(left[at, :], right[...]).astype(bf16)
            for b in range(ny):
                s = t * ny + b

                @pl.when(s != me_k)
                def _():
                    kv_block(j, s, me_k).start()

            return carry

        lax.fori_loop(first, end, step, 0)

    def summed(ref):
        acc = ref[0].astype(f32)
        for s in range(1, ref.shape[0]):
            acc = acc + ref[s].astype(f32)
        return acc

    def g_block(j, s, device, sem, n):
        ref = gr.at[s, 0:tok, 128 * j : 128 * j + 128]
        return send(ref, ref, sem.at[j, n], p_recv.at[j, s], device)

    def grad_out(j):
        src = gr.at[me_p, 0:tok, 128 * j : 128 * j + 128]
        return pltpu.make_async_copy(src, (dq_out, dk_out, dv_out)[j], out_sem.at[j])

    def send_grad(j, ref):
        gr[me_p, 0:tok, 128 * j : 128 * j + 128] = summed(ref).astype(bf16)
        each_y(lambda b: g_block(j, me_p, (x, zl, zh, b, c), p_send, b).start())
        g_block(j, me_p, partner, h_send, y).start()
        grad_out(j).start()

    def w_block(j, s, n):
        return send(ws.at[j, s], wr.at[j, n], w_send.at[j, s], w_recv.at[j, n], at_zh(s))

    def send_weight(j):
        def land(b):
            s = b * nc + c
            g_block(j, s, partner, h_send, b).wait_recv()
            g_block(j, s, partner, h_send, b).start()

        each_y(land)

        def land_rest(b, carry):
            g_block(j, b * nc + other, partner, h_send, b).wait_recv()
            return carry

        lax.fori_loop(0, ny, land_rest, 0)
        acc = dot(xr[0], gr[0, :, 128 * j : 128 * j + 128])
        for p in range(1, npc):
            acc = acc + dot(xr[p], gr[p, :, 128 * j : 128 * j + 128])
        for n in range(nzh):
            ws[j, n] = acc[n * chunk : (n + 1) * chunk, :].astype(bf16)
        each(zh, nzh, lambda s: w_block(j, s, zh).start())
        wr[j, zh] = ws[j, zh]

    def a_block(j, s, n):
        return send(ar.at[j, n], ar.at[j, n], a_send.at[j, s], a_recv.at[j, n], at_r(s))

    def send_rows(j):
        each(zh, nzh, lambda s: w_block(j, s, s).wait_recv())
        ar[j, me_r] = summed(wr.at[j]).astype(bf16)
        each(me_r, nr, lambda s: a_block(j, s, me_r).start())

    def weight_out(j):
        lanes = slice(128 * j, 128 * j + 128)
        return pltpu.make_async_copy(wg.at[:, lanes], wg_out.at[:, lanes], out_sem.at[3 + j])

    def finish(j):
        each(me_r, nr, lambda s: a_block(j, s, s).wait_recv())
        wg[:, 128 * j : 128 * j + 128] = summed(ar.at[j])
        weight_out(j).start()

    grad_tiles(1, 0, 1)
    send_dq()
    grad_tiles(1, 1, nx)
    dvr[me_k] = dvs[mine_k, :]
    grad_tiles(0, 0, nx)
    dkr[me_k] = dks[mine_k, :]
    each_z(lambda w: dq_block(w, w).wait_recv())
    send_grad(0, dqr)
    own.wait()
    each(me_p, npc, lambda s: x_block(s, s).wait_recv())
    each(me_k, nk, lambda s: kv_block(1, s, s).wait_recv())
    send_grad(2, dvr)
    send_weight(0)
    each(me_k, nk, lambda s: kv_block(0, s, s).wait_recv())
    send_grad(1, dkr)
    send_weight(2)
    send_rows(0)
    send_weight(1)
    send_rows(2)
    finish(0)
    send_rows(1)
    finish(2)
    finish(1)

    for m in range(3):
        each_z(lambda w: q_block(m, me_q, partner, q_send, w).wait_send())

        def f_left(w, carry):
            q_block(m, me_q, partner, f_send, w).wait_send()
            return carry

        lax.fori_loop(0, nz, f_left, 0)

    def st_left(s):
        for h in range(2):
            st_block(h, me_q, partner, s).wait_send()

    each(me_q, nq, st_left)

    def pair_left(w, carry):
        pair_block(w, other).wait_send()
        return carry

    lax.fori_loop(0, nz, pair_left, 0)
    each_z(lambda w: dq_block(w, z).wait_send())

    def k_left(s):
        for j in range(2):
            k_block(j, me_k, partner, s).wait_send()
            kv_block(j, s, me_k).wait_send()

    each(me_k, nk, k_left)
    each(me_p, npc, lambda s: x_block(s, me_p).wait_send())

    for j in range(3):
        each_y(lambda b: g_block(j, me_p, partner, p_send, b).wait_send())

        def h_left(b, carry):
            g_block(j, me_p, partner, h_send, b).wait_send()
            return carry

        lax.fori_loop(0, ny, h_left, 0)
        each(zh, nzh, lambda s: w_block(j, s, zh).wait_send())
        each(me_r, nr, lambda s: a_block(j, s, me_r).wait_send())
        grad_out(j).wait()
        weight_out(j).wait()


def local(
    dims, layer_input, queries, key_states, value_states, forward_out, out_grad, token_pos,
    block_sample,
):
    nx, nzl, nzh, ny, nc = dims
    tok = queries.shape[0]
    depth = layer_input.shape[1]
    chunk = depth // (nzh * ny * nc)
    nq, nk, npc, nr = nzh * nzl * nc, nx * ny, ny * nc, nx * nzl
    n_query, n_key = nq * tok, nk * tok
    pos = token_pos.reshape(-1, 128)
    nz = nzh * nzl
    V = pltpu.VMEM
    dma = pltpu.SemaphoreType.DMA
    scratch = [
        V((n_query, 128), bf16), V((n_query, 128), bf16), V((tok, 128), bf16), V((nq, 1, 256), f32),
        V((n_key, 128), bf16), V((n_key, 128), bf16), V((tok, depth), bf16),
        V(pos.shape, jnp.int32), pltpu.SMEM(block_sample.shape, jnp.int32), V((256, 128), f32),
        V((n_query, 128), bf16), V((n_key, 128), bf16), V((128, n_key), bf16),
        V((n_key, n_query), bf16), V((n_key, n_query), bf16), V((n_key, 256), f32),
        V((128, n_query), f32), V((2, nq, 2, n_query // 2), f32), V((8, n_query), f32),
        V((n_query, 128), bf16), V((n_query, 128), bf16),
        V((n_query, 128), bf16), V((nz, tok, 128), bf16), V((nz, tok, 128), bf16),
        V((nz, tok, 128), bf16),
        V((n_key, 128), bf16), V((n_key, 128), bf16),
        V((nk, tok, 128), bf16), V((nk, tok, 128), bf16),
        V((npc, nzh * chunk, 256), bf16), V((npc, nzh * chunk, 256), bf16),
        V((npc, 256, 384), bf16), V((3, nzh, chunk, 128), bf16), V((3, nzh, chunk, 128), bf16),
        V((3, nr, chunk, 128), bf16), V((chunk, 384), f32),
        dma((3, nz)), dma((3, nq)), dma((3, nz)), dma((2, nq)), dma((2, nq)),
        dma((nz,)), dma((nz,)), dma((nz,)), dma((nz,)),
        dma((4, nk)), dma((4, nk)), dma((npc,)), dma((npc,)),
        dma((3, ny)), dma((3, ny)), dma((3, npc)),
        dma((3, nzh)), dma((3, nzh)), dma((3, nr)), dma((3, nr)), dma, dma((8,)), dma((6,)),
    ]

    def body(*refs):
        kernel(dims, *refs)

    hbm = pl.BlockSpec(memory_space=pl.ANY)
    grad = jax.ShapeDtypeStruct((tok, 128), bf16)
    return pl.pallas_call(
        body,
        out_shape=(grad, grad, grad, jax.ShapeDtypeStruct((chunk, 384), f32)),
        in_specs=[hbm] * 8,
        out_specs=(hbm,) * 4,
        scratch_shapes=scratch,
        compiler_params=pltpu.CompilerParams(
            collective_id=0, has_side_effects=True, vmem_limit_bytes=64 * 2**20
        ),
        name="packed_backward",
    )(queries, key_states, value_states, forward_out, out_grad, layer_input, pos, block_sample)


def on_mesh(finer):
    dims = tuple(finer.shape[a] for a in AXES)
    slots, cols = P(AXES, None), P(("zh", "y", "c"), None)
    return jax.shard_map(
        lambda *args: local(dims, *args),
        mesh=finer,
        in_specs=(slots,) * 6 + (P(), P()),
        out_specs=(slots, slots, slots, cols),
        check_vma=False,
    )


def solution(mesh):
    return on_mesh(Mesh(mesh.devices.reshape(4, 2, 4, 4, 2), AXES))
```

time: 109 us -> 104 us (0.954)
  local copies, waits for them, and re-layouts: 7.88 us -> 4.89 us
  Pallas kernels: 100 us -> 97.8 us
    reshape x2 -> x0, local copies, waits for them, and re-layouts: 2.98 us -> none  [the longest x1 1.74 us: local(): pos = token_pos.reshape(-1, tok)]
    pallas_call x1, Pallas kernels: 100 us -> 97.8 us  [local(): pl.pallas_call(body, out_shape=(grad, grad, grad, jax.ShapeDtypeStruct((c...]
where the time goes in v3:
time: 104 us; the launch traced here: 103 us
  Pallas kernels  97.8 us (94%)
  local copies, waits for them, and re-layouts  4.89 us (5%)
    pallas_call x1, Pallas kernels, local(): pl.pallas_call(body, out_shape=(grad, grad, grad, jax.ShapeDtypeStruct((c...  97.8 us
    unnamed x6, local copies, waits for them, and re-layouts  4.89 us

profile of v3, /device:TPU:1, one launch (start us, length us, event | category | flops | bytes accessed | tf_op | source)
XLA Modules:
  0.0 103.3 jit_solution(16427937919091380395)
XLA Ops:
  0.6 97.8 %packed_backward.1 = (bf16[160,128]{1,0:T(8,128)(2,1)}, bf16[160,128]{1,0:T(8,128)(2,1)}, bf16[160,128]{1,0:T(8,128)(2,1)}, f32[96,384]{1,0:T(8,128)}) custom-call(bf16[160,128]{1,0:T(8,128)(2,1)} %refs_0_.1, bf16[160,128]{1,0:T(8,128)(2,1)} %refs_1_.1, bf16[160,128]{1,0:T(8,128)(2,1)} %refs_2_.1, bf16[160,128]{1,0:T(8,128)(2,1)} %refs_3_.1, ...), custom_call_target="tpu_custom_call" | custom-call | tf_op jit(solution)/shard_map/packed_backward/pallas_call | solution.py:550
  98.4 0.0 copy-start
  98.5 1.4 %copy.16 = bf16[160,128]{1,0:T(8,128)(2,1)} copy(bf16[160,128]{1,0:T(8,128)(2,1)} %get-tuple-element.8) | data formatting | bytes 81920
  99.9 1.4 %copy.17 = bf16[160,128]{1,0:T(8,128)(2,1)} copy(bf16[160,128]{1,0:T(8,128)(2,1)} %get-tuple-element.9) | data formatting | bytes 81920
  101.3 1.4 %copy.18 = bf16[160,128]{1,0:T(8,128)(2,1)} copy(bf16[160,128]{1,0:T(8,128)(2,1)} %get-tuple-element.10) | data formatting | bytes 81920
  102.7 0.0 copy-done
  102.7 0.7 copy.19
Async XLA Ops:
  98.4 4.2 %copy-start = (f32[96,384]{1,0:T(8,128)S(1)}, f32[96,384]{1,0:T(8,128)}, u32[]{:S(2)}) copy-start(f32[96,384]{1,0:T(8,128)} %get-tuple-element.11) | copy-start | bytes 442372

commit v4 on v3

--- a/solution.py
+++ b/solution.py
@@ -39,12 +39,17 @@
     return sorted(range(1, n), key=lambda d: -min(d, n - d))
 
 
+def near(i):
+    return i + i // 2 - 2 * (i // 3)
+
+
 def kernel(
     dims, q_in, k_in, v_in, o_in, g_in, x_in, pos_ref, block_ref,
     dq_out, dk_out, dv_out, wg_out,
-    qb, gb, ob, db, kb, vb, xb, pos, blocks, column, fq, fk, kt, et, ut, s_scr, dqt, st, rr, gs, qs,
+    qb, gb, ob, db, kb, vb, xb, pos, blocks, column, fq, fk, kt, et, ut, s_scr, dqt, st, pk, lk, wk, rr,
+    gs, qs,
     dqs, dqp, dqc, dqr, dks, dvs, dkr, dvr, xt, xr, gr, ws, wr, ar, wg,
-    q_send, q_recv, f_send, t_send, t_recv, e_send, e_recv, d_send, d_recv, k_send, k_recv,
+    q_send, q_recv, f_send, e_send, e_recv, d_send, d_recv, k_send, k_recv,
     x_send, x_recv, p_send, h_send, p_recv, w_send, w_recv, a_send, a_recv, own_sem, in_sem, out_sem,
 ):
     nx, nzl, nzh, ny, nc = dims
@@ -60,7 +65,7 @@
     me_p = y * nc + c
     me_r = x * nzl + zl
     n_query, n_key = nq * tok, nk * tok
-    half = n_query // 2
+    key_chunk, query_chunk = ny * tok, nzl * nc * tok
 
     def rows_of(s):
         return pl.ds(pl.multiple_of(s * tok, tok), tok)
@@ -105,9 +110,19 @@
             body(lax.rem(y + d, ny))
 
     def each_xy(body):
-        pairs = [(a, b) for a in range(nx) for b in range(ny) if a or b]
-        for a, b in sorted(pairs, key=lambda p: -min(p[0], nx - p[0]) - min(p[1], ny - p[1])):
-            body(lax.rem(x + a, nx), lax.rem(y + b, ny))
+        for i in range(nx):
+            for n in range(ny):
+                if i or n:
+                    body(lax.rem(x + nx - near(i), nx), lax.rem(y + ny - near(n), ny))
+
+    def chunk_z(i, body):
+        h = lax.rem(zh + near(i), nzh)
+        for n in range(nzl):
+            w = h * nzl + n
+            if i:
+                body(w)
+            else:
+                pl.when(w != z)(lambda w=w: body(w))
 
     mine_q, mine_k = rows_of(me_q), rows_of(me_k)
     staged = [
@@ -141,7 +156,7 @@
     pl.semaphore_wait(barrier, nq + nk + npc + nzh + nr - 5)
 
     def q_block(m, s, device, sem, n):
-        ref = (qb.at[rows_of(s), :], gb.at[rows_of(s), :], db.at[s])[m]
+        ref = (qb.at[rows_of(s), :], gb.at[rows_of(s), :], db.at[s], st.at[s])[m]
         return send(ref, ref, sem.at[m, n], q_recv.at[m, s], device)
 
     def k_block(m, s, device, n):
@@ -149,29 +164,40 @@
         return send(ref, ref, k_send.at[m, n], k_recv.at[m, s], device)
 
     def start_q(m):
-        each_z(lambda w: q_block(m, me_q, at_z(w, c), q_send, w).start())
+        for i in range(nzh):
+            h = lax.rem(zh + nzh - near(i), nzh)
+            for n in range(nzl):
+                w = h * nzl + n
+                copy = q_block(m, me_q, at_z(w, c), q_send, w)
+                if i:
+                    copy.start()
+                else:
+                    pl.when(w != z)(copy.start)
         q_block(m, me_q, partner, f_send, z).start()
 
     def start_k(m):
         each_xy(lambda a, b: k_block(m, me_k, at_xy(a, b), a * ny + b).start())
 
-    def hand_on(m):
+    def hand_on(m, i):
         def land(w):
             s = w * nc + c
             q_block(m, s, partner, f_send, w).wait_recv()
             q_block(m, s, partner, f_send, w).start()
 
-        each_z(land)
-
-    def land_q(m):
-        def land(w, carry):
+        chunk_z(i, land)
+
+    def land_q(m, i):
+        h = lax.rem(zh + near(i), nzh)
+        for n in range(nzl):
+            w = h * nzl + n
             q_block(m, w * nc + other, partner, f_send, w).wait_recv()
-            return carry
-
-        lax.fori_loop(0, nz, land, 0)
-
-    def land_k(m):
-        each_xy(lambda a, b: k_block(m, a * ny + b, at_xy(a, b), a * ny + b).wait_recv())
+
+    def land_k(m, i):
+        a = lax.rem(x + near(i), nx)
+        for n in range(ny):
+            if i or n:
+                s = a * ny + lax.rem(y + near(n), ny)
+                k_block(m, s, partner, s).wait_recv()
 
     start_q(0)
     start_k(0)
@@ -217,7 +243,6 @@
 
     lax.fori_loop(0, nk, key_hot, 0)
 
-    hand_on(0)
     lax.fori_loop(0, nq, query_hot, 0)
 
     xt[:, :, tok:] = jnp.zeros((npc, nzh * chunk, 256 - tok), bf16)
@@ -230,74 +255,114 @@
             rows = slice(n // npc * chunk, (n // npc + 1) * chunk)
             xt[n % npc, rows, 0:tok] = turned[j * chunk : (j + 1) * chunk, :]
 
-    land_k(0)
-    land_q(0)
-
     def x_block(s, n):
         return send(xt.at[s], xr.at[n], x_send.at[s], x_recv.at[n], at_p(s))
 
     own = pltpu.make_async_copy(xt.at[me_p], xr.at[me_p], own_sem)
     own.start()
-    each(me_p, npc, lambda s: x_block(s, me_p).start())
-
-    tq = 256 if half % 256 == 0 else 128
-    tk = 256 if n_key % 256 == 0 else tok
+
+    tq = 256
     score_scale = 1.0 / math.sqrt(128.0)
     rate = score_scale / math.log(2.0)
-    kt[...] = dot_nt(eye(128), kb[...]).astype(bf16)
-
     def tile(t):
         return pl.ds(pl.multiple_of(t * tq, tq), tq)
 
-    def score_tile(t):
-        at = tile(t)
+    def sweep(moved, block):
+        @pl.loop(0, nx * nx)
+        def _(t):
+            for i in range(nx):
+
+                @pl.when(t == i * i)
+                def _():
+                    for m in moved:
+                        hand_on(m, i)
+                    land_k(moved[0], i)
+
+                @pl.when(t == i * i + i)
+                def _():
+                    for m in moved:
+                        land_q(m, i)
+
+            shell = sum(jnp.where(t >= i * i, 1, 0) for i in range(1, nx))
+            rest = t - shell * shell
+            inner = rest < shell
+            ki, qi = jnp.where(inner, shell, rest - shell), jnp.where(inner, rest, shell)
+            block(lax.rem(x + near(ki), nx), lax.rem(zh + near(qi), nzh), t)
+
+    def chunk_rows(n, size):
+        return pl.ds(pl.multiple_of(n * size, size), size)
+
+    def score_block(kc, qc, t):
+        span, at = chunk_rows(kc, key_chunk), chunk_rows(qc, query_chunk)
         query_tile = jnp.concatenate([qb[at, :], fq[at, :]], axis=1)
-        top = jnp.full((8, tq), -3.0e38, f32)
-        for n in range(n_key // tk):
-            span = slice(n * tk, (n + 1) * tk)
-            s = dot_nt(jnp.concatenate([kb[span, :], fk[span, :]], axis=1), query_tile)
-            s_scr[span, 0:tq] = s
-            top = jnp.maximum(top, jnp.max(s.reshape(tk // 8, 8, tq), axis=0))
+        s = dot_nt(jnp.concatenate([kb[span, :], fk[span, :]], axis=1), query_tile)
+        s_scr[...] = s
+        top = jnp.max(s.reshape(key_chunk // 8, 8, query_chunk), axis=0)
         peak = jnp.max(top, axis=0, keepdims=True)
-        total = jnp.zeros((8, tq), f32)
-        for n in range(n_key // tk):
-            span = slice(n * tk, (n + 1) * tk)
-            e = jnp.exp2((s_scr[span, 0:tq] - peak) * rate)
-            total = total + jnp.sum(e.reshape(tk // 8, 8, tq), axis=0)
-            et[span, at] = e.astype(bf16)
-        rr[0:1, at] = peak
-        rr[1:2, at] = jnp.sum(total, axis=0, keepdims=True)
-
-    def grad_tile(t):
-        at = tile(t)
-        grad_rows = gb[at, :]
-        delta_row = rr[2:3, at]
-        acc = jnp.zeros((128, tq), f32)
-        for n in range(n_key // tk):
-            span = slice(n * tk, (n + 1) * tk)
-            slope = dot_nt(vb[span, :], grad_rows) - delta_row
-            u = (et[span, at].astype(f32) * slope).astype(bf16)
-            ut[span, at] = u
-            acc = acc + dot(kt[:, span], u)
-        dqt[:, at] = acc
-
-    def st_block(h, s, device, n):
-        return send(st.at[h, s], st.at[h, s], t_send.at[h, n], t_recv.at[h, s], device)
-
-    def send_stats(h):
-        st[h, me_q] = rr[0:2, h * half : (h + 1) * half]
-        each(me_q, nq, lambda s: st_block(h, me_q, at_z(s // nc, lax.rem(s, nc)), s).start())
-
-    def factors(h):
-        each(me_q, nq, lambda s: st_block(h, s, partner, s).wait_recv())
-        part = slice(h * half, (h + 1) * half)
-        peak = st[h, 0, 0:1, :]
-        for s in range(1, nq):
-            peak = jnp.maximum(peak, st[h, s, 0:1, :])
-        total = jnp.zeros_like(peak)
-        for s in range(nq):
-            total = total + st[h, s, 1:2, :] * jnp.exp2((st[h, s, 0:1, :] - peak) * rate)
-        rr[3:4, part] = jnp.exp2((rr[0:1, part] - peak) * rate) / total
+        e = jnp.exp2((s_scr[...] - peak) * rate)
+        total = jnp.sum(e.reshape(key_chunk // 8, 8, query_chunk), axis=0)
+        et[span, at] = e.astype(bf16)
+        pk[kc, :, at] = peak
+        lk[kc, :, at] = jnp.sum(total, axis=0, keepdims=True)
+
+    def grad_block(kc, qc, t):
+        span, at = chunk_rows(kc, key_chunk), chunk_rows(qc, query_chunk)
+        for i in range(nx):
+
+            @pl.when(t == i * i + i)
+            def _():
+                rows = [db[qc * nzl * nc + n, :, 0:tok] for n in range(nzl * nc)]
+                rr[2:3, at] = jnp.concatenate(rows, axis=1)
+
+        @pl.when(t == nx * nx - 3)
+        def _():
+            for i in range(nzh):
+                hand_on(3, i)
+
+        values, turned = vb[span, :], kt[kc]
+        for first in range(0, query_chunk, tq):
+            wide = min(tq, query_chunk - first)
+            part = pl.ds(pl.multiple_of(qc * query_chunk + first, 128), wide)
+            slope = dot_nt(values, gb[part, :]) - rr[2:3, part]
+            e = et[span, part].astype(f32) * wk[kc, :, part]
+            u = (e * slope).astype(bf16)
+            et[span, part] = e.astype(bf16)
+            ut[span, part] = u
+            dqt[:, part] += dot(turned, u)
+
+    sweep((0,), score_block)
+
+    peak = pk[0]
+    for n in range(1, nx):
+        peak = jnp.maximum(peak, pk[n])
+    total = jnp.zeros_like(peak)
+    for n in range(nx):
+        weight = jnp.exp2((pk[n] - peak) * rate)
+        wk[n] = weight
+        total = total + lk[n] * weight
+    rr[0:1, :] = peak
+    rr[1:2, :] = total
+    st[me_q] = rr[0:2, :]
+    start_q(3)
+
+    def x_block(s, n):
+        return send(xt.at[s], xr.at[n], x_send.at[s], x_recv.at[n], at_p(s))
+
+    each(me_p, npc, lambda s: x_block(s, me_p).start())
+    for n in range(nx):
+        kt[n] = dot_nt(eye(128), kb[n * key_chunk : (n + 1) * key_chunk, :]).astype(bf16)
+    dqt[...] = jnp.zeros_like(dqt)
+    sweep((1, 2), grad_block)
+    for i in range(nzh):
+        land_q(3, i)
+
+    peak = st[0, 0:1, :]
+    for s in range(1, nq):
+        peak = jnp.maximum(peak, st[s, 0:1, :])
+    total = jnp.zeros_like(peak)
+    for s in range(nq):
+        total = total + st[s, 1:2, :] * jnp.exp2((st[s, 0:1, :] - peak) * rate)
+    rr[3:4, :] = jnp.exp2((rr[0:1, :] - peak) * rate) / total
 
     def scale_rows(t):
         at = tile(t)
@@ -307,23 +372,7 @@
         gs[at, :] = (gb[at, :].astype(f32) * col).astype(bf16)
         qs[at, :] = (qb[at, :].astype(f32) * (col * score_scale)).astype(bf16)
 
-    tiles = n_query // tq
-    most = tiles - max(1, tiles // 5)
-    pl.loop(0, tiles // 2)(score_tile)
-    send_stats(0)
-    pl.loop(tiles // 2, most)(score_tile)
-    hand_on(2)
-    hand_on(1)
-    pl.loop(most, tiles)(score_tile)
-    send_stats(1)
-    land_k(1)
-    land_q(2)
-    land_q(1)
-    rr[2:3, :] = jnp.concatenate([db[s, :, 0:tok] for s in range(nq)], axis=1)
-    pl.loop(0, tiles)(grad_tile)
-    factors(0)
-    factors(1)
-    pl.loop(0, tiles)(scale_rows)
+    pl.loop(0, n_query // tq)(scale_rows)
 
     def pair_block(w, core):
         src = dqs.at[rows_of(w * nc + core), :]
@@ -462,7 +511,7 @@
     finish(2)
     finish(1)
 
-    for m in range(3):
+    for m in range(4):
         each_z(lambda w: q_block(m, me_q, partner, q_send, w).wait_send())
 
         def f_left(w, carry):
@@ -470,12 +519,6 @@
             return carry
 
         lax.fori_loop(0, nz, f_left, 0)
-
-    def st_left(s):
-        for h in range(2):
-            st_block(h, me_q, partner, s).wait_send()
-
-    each(me_q, nq, st_left)
 
     def pair_left(w, carry):
         pair_block(w, other).wait_send()
@@ -504,6 +547,20 @@
         each(me_r, nr, lambda s: a_block(j, s, me_r).wait_send())
         grad_out(j).wait()
         weight_out(j).wait()
+
+
+def hand_out(*refs):
+    count = len(refs) // 3
+    sources, results, held, sems = refs[:count], refs[count : 2 * count], refs[2 * count : -1], refs[-1]
+    into = [pltpu.make_async_copy(sources[i], held[i], sems.at[0, i]) for i in range(count)]
+    out = [pltpu.make_async_copy(held[i], results[i], sems.at[1, i]) for i in range(count)]
+    for copy in into:
+        copy.start()
+    for i in range(count):
+        into[i].wait()
+        out[i].start()
+    for copy in out:
+        copy.wait()
 
 
 def local(
@@ -524,9 +581,10 @@
         V((n_query, 128), bf16), V((n_query, 128), bf16), V((tok, 128), bf16), V((nq, 1, 256), f32),
         V((n_key, 128), bf16), V((n_key, 128), bf16), V((tok, depth), bf16),
         V(pos.shape, jnp.int32), pltpu.SMEM(block_sample.shape, jnp.int32), V((256, 128), f32),
-        V((n_query, 128), bf16), V((n_key, 128), bf16), V((128, n_key), bf16),
-        V((n_key, n_query), bf16), V((n_key, n_query), bf16), V((n_key, 256), f32),
-        V((128, n_query), f32), V((2, nq, 2, n_query // 2), f32), V((8, n_query), f32),
+        V((n_query, 128), bf16), V((n_key, 128), bf16), V((nx, 128, ny * tok), bf16),
+        V((n_key, n_query), bf16), V((n_key, n_query), bf16), V((ny * tok, nzl * nc * tok), f32),
+        V((128, n_query), f32), V((nq, 2, n_query), f32),
+        V((nx, 1, n_query), f32), V((nx, 1, n_query), f32), V((nx, 1, n_query), f32), V((8, n_query), f32),
         V((n_query, 128), bf16), V((n_query, 128), bf16),
         V((n_query, 128), bf16), V((nz, tok, 128), bf16), V((nz, tok, 128), bf16),
         V((nz, tok, 128), bf16),
@@ -535,7 +593,7 @@
         V((npc, nzh * chunk, 256), bf16), V((npc, nzh * chunk, 256), bf16),
         V((npc, 256, 384), bf16), V((3, nzh, chunk, 128), bf16), V((3, nzh, chunk, 128), bf16),
         V((3, nr, chunk, 128), bf16), V((chunk, 384), f32),
-        dma((3, nz)), dma((3, nq)), dma((3, nz)), dma((2, nq)), dma((2, nq)),
+        dma((4, nz)), dma((4, nq)), dma((4, nz)),
         dma((nz,)), dma((nz,)), dma((nz,)), dma((nz,)),
         dma((4, nk)), dma((4, nk)), dma((npc,)), dma((npc,)),
         dma((3, ny)), dma((3, ny)), dma((3, npc)),
@@ -547,9 +605,10 @@
 
     hbm = pl.BlockSpec(memory_space=pl.ANY)
     grad = jax.ShapeDtypeStruct((tok, 128), bf16)
-    return pl.pallas_call(
+    shapes = (grad, grad, grad, jax.ShapeDtypeStruct((chunk, 384), f32))
+    results = pl.pallas_call(
         body,
-        out_shape=(grad, grad, grad, jax.ShapeDtypeStruct((chunk, 384), f32)),
+        out_shape=shapes,
         in_specs=[hbm] * 8,
         out_specs=(hbm,) * 4,
         scratch_shapes=scratch,
@@ -558,6 +617,14 @@
         ),
         name="packed_backward",
     )(queries, key_states, value_states, forward_out, out_grad, layer_input, pos, block_sample)
+    return pl.pallas_call(
+        hand_out,
+        out_shape=shapes,
+        in_specs=[hbm] * 4,
+        out_specs=(hbm,) * 4,
+        scratch_shapes=[V(a.shape, a.dtype) for a in shapes] + [dma((2, 4))],
+        name="hand_out",
+    )(*results)
 
 
 def on_mesh(finer):

time: 104 us -> 108 us (1.038)
  Pallas kernels: 97.8 us -> 107 us
  local copies, waits for them, and re-layouts: 4.89 us -> 0 us
    pallas_call x1 -> x2, Pallas kernels: 97.8 us -> 107 us  [the longest x1 105 us: local(): pl.pallas_call(body, out_shape=shapes, in_specs=[hbm] * 8, out_specs=(hbm...]
    unnamed x6 -> x0, local copies, waits for them, and re-layouts: 4.89 us -> none
where the time goes in v4:
time: 108 us; the launch traced here: 107 us
  Pallas kernels  107 us (99%)
    pallas_call x1, Pallas kernels, local(): pl.pallas_call(body, out_shape=shapes, in_specs=[hbm] * 8, out_specs=(hbm...  105 us

profile of v4, /device:TPU:1, one launch (start us, length us, event | category | flops | bytes accessed | tf_op | source)
XLA Modules:
  0.0 107.2 jit_solution(400359976318687720)
XLA Ops:
  0.6 104.9 %packed_backward.1 = (bf16[160,128]{1,0:T(8,128)(2,1)}, bf16[160,128]{1,0:T(8,128)(2,1)}, bf16[160,128]{1,0:T(8,128)(2,1)}, f32[96,384]{1,0:T(8,128)}) custom-call(bf16[160,128]{1,0:T(8,128)(2,1)} %refs_0_.1, bf16[160,128]{1,0:T(8,128)(2,1)} %refs_1_.1, bf16[160,128]{1,0:T(8,128)(2,1)} %refs_2_.1, bf16[160,128]{1,0:T(8,128)(2,1)} %refs_3_.1, ...), custom_call_target="tpu_custom_call" | custom-call | tf_op jit(solution)/shard_map/packed_backward/pallas_call | solution.py:609
  105.5 1.7 %hand_out.1 = (bf16[160,128]{1,0:T(8,128)(2,1)}, bf16[160,128]{1,0:T(8,128)(2,1)}, bf16[160,128]{1,0:T(8,128)(2,1)}, f32[96,384]{1,0:T(8,128)}) custom-call(bf16[160,128]{1,0:T(8,128)(2,1)} %get-tuple-element.8.refs_0_, bf16[160,128]{1,0:T(8,128)(2,1)} %get-tuple-element.9.refs_1_, bf16[160,128]{1,0:T(8,128)(2,1)} %get-tuple-element.10.refs_2_, ...), custom_call_target="tpu_custom_call" | custom-call | tf_op jit(solution)/shard_map/hand_out/pallas_call | solution.py:620

commit v5 on v4

--- a/solution.py
+++ b/solution.py
@@ -201,9 +201,6 @@
 
     start_q(0)
     start_k(0)
-    start_q(2)
-    start_q(1)
-    start_k(1)
 
     for copy in staged[5:]:
         copy.wait()
@@ -293,6 +290,12 @@
         return pl.ds(pl.multiple_of(n * size, size), size)
 
     def score_block(kc, qc, t):
+        @pl.when(t == min(3, nx * nx - 1))
+        def _():
+            start_q(2)
+            start_q(1)
+            start_k(1)
+
         span, at = chunk_rows(kc, key_chunk), chunk_rows(qc, query_chunk)
         query_tile = jnp.concatenate([qb[at, :], fq[at, :]], axis=1)
         s = dot_nt(jnp.concatenate([kb[span, :], fk[span, :]], axis=1), query_tile)
@@ -319,7 +322,7 @@
             for i in range(nzh):
                 hand_on(3, i)
 
-        values, turned = vb[span, :], kt[kc]
+        values = vb[span, :]
         for first in range(0, query_chunk, tq):
             wide = min(tq, query_chunk - first)
             part = pl.ds(pl.multiple_of(qc * query_chunk + first, 128), wide)
@@ -328,7 +331,6 @@
             u = (e * slope).astype(bf16)
             et[span, part] = e.astype(bf16)
             ut[span, part] = u
-            dqt[:, part] += dot(turned, u)
 
     sweep((0,), score_block)
 
@@ -349,10 +351,15 @@
         return send(xt.at[s], xr.at[n], x_send.at[s], x_recv.at[n], at_p(s))
 
     each(me_p, npc, lambda s: x_block(s, me_p).start())
-    for n in range(nx):
-        kt[n] = dot_nt(eye(128), kb[n * key_chunk : (n + 1) * key_chunk, :]).astype(bf16)
-    dqt[...] = jnp.zeros_like(dqt)
+    kt[...] = dot_nt(eye(128), kb[...]).astype(bf16)
     sweep((1, 2), grad_block)
+    wide = 512 if n_query % 512 == 0 else tq
+
+    @pl.loop(0, n_query // wide)
+    def _(t):
+        at = pl.ds(pl.multiple_of(t * wide, wide), wide)
+        dqt[:, at] = dot(kt[...], ut[:, at])
+
     for i in range(nzh):
         land_q(3, i)
 
@@ -581,7 +588,7 @@
         V((n_query, 128), bf16), V((n_query, 128), bf16), V((tok, 128), bf16), V((nq, 1, 256), f32),
         V((n_key, 128), bf16), V((n_key, 128), bf16), V((tok, depth), bf16),
         V(pos.shape, jnp.int32), pltpu.SMEM(block_sample.shape, jnp.int32), V((256, 128), f32),
-        V((n_query, 128), bf16), V((n_key, 128), bf16), V((nx, 128, ny * tok), bf16),
+        V((n_query, 128), bf16), V((n_key, 128), bf16), V((128, n_key), bf16),
         V((n_key, n_query), bf16), V((n_key, n_query), bf16), V((ny * tok, nzl * nc * tok), f32),
         V((128, n_query), f32), V((nq, 2, n_query), f32),
         V((nx, 1, n_query), f32), V((nx, 1, n_query), f32), V((nx, 1, n_query), f32), V((8, n_query), f32),

time: 108 us -> 100 us (0.926)
  Pallas kernels: 107 us -> 99.5 us
    pallas_call x1, Pallas kernels: 105 us -> 97.7 us  [local(): pl.pallas_call(body, out_shape=shapes, in_specs=[hbm] * 8, out_specs=(hbm...]
where the time goes in v5:
time: 100 us
  Pallas kernels  99.5 us (100%)
    pallas_call x1, Pallas kernels, local(): pl.pallas_call(body, out_shape=shapes, in_specs=[hbm] * 8, out_specs=(hbm...  97.7 us

profile of v5, /device:TPU:1, one launch (start us, length us, event | category | flops | bytes accessed | tf_op | source)
XLA Modules:
  0.0 100.1 jit_solution(8782618831969377350)
XLA Ops:
  0.6 97.7 %packed_backward.1 = (bf16[160,128]{1,0:T(8,128)(2,1)}, bf16[160,128]{1,0:T(8,128)(2,1)}, bf16[160,128]{1,0:T(8,128)(2,1)}, f32[96,384]{1,0:T(8,128)}) custom-call(bf16[160,128]{1,0:T(8,128)(2,1)} %refs_0_.1, bf16[160,128]{1,0:T(8,128)(2,1)} %refs_1_.1, bf16[160,128]{1,0:T(8,128)(2,1)} %refs_2_.1, bf16[160,128]{1,0:T(8,128)(2,1)} %refs_3_.1, ...), custom_call_target="tpu_custom_call" | custom-call | tf_op jit(solution)/shard_map/packed_backward/pallas_call | solution.py:616
  98.4 1.7 %hand_out.1 = (bf16[160,128]{1,0:T(8,128)(2,1)}, bf16[160,128]{1,0:T(8,128)(2,1)}, bf16[160,128]{1,0:T(8,128)(2,1)}, f32[96,384]{1,0:T(8,128)}) custom-call(bf16[160,128]{1,0:T(8,128)(2,1)} %get-tuple-element.8.refs_0_, bf16[160,128]{1,0:T(8,128)(2,1)} %get-tuple-element.9.refs_1_, bf16[160,128]{1,0:T(8,128)(2,1)} %get-tuple-element.10.refs_2_, ...), custom_call_target="tpu_custom_call" | custom-call | tf_op jit(solution)/shard_map/hand_out/pallas_call | solution.py:627

commit v6 on v5

--- a/solution.py
+++ b/solution.py
@@ -242,22 +242,6 @@
 
     lax.fori_loop(0, nq, query_hot, 0)
 
-    xt[:, :, tok:] = jnp.zeros((npc, nzh * chunk, 256 - tok), bf16)
-    gr[:, tok:, :] = jnp.zeros((npc, 256 - tok, 384), bf16)
-    four = eye(4 * chunk)
-    for g in range(nzh * npc // 4):
-        turned = dot_nt(four, xb[:, g * 4 * chunk : (g + 1) * 4 * chunk]).astype(bf16)
-        for j in range(4):
-            n = 4 * g + j
-            rows = slice(n // npc * chunk, (n // npc + 1) * chunk)
-            xt[n % npc, rows, 0:tok] = turned[j * chunk : (j + 1) * chunk, :]
-
-    def x_block(s, n):
-        return send(xt.at[s], xr.at[n], x_send.at[s], x_recv.at[n], at_p(s))
-
-    own = pltpu.make_async_copy(xt.at[me_p], xr.at[me_p], own_sem)
-    own.start()
-
     tq = 256
     score_scale = 1.0 / math.sqrt(128.0)
     rate = score_scale / math.log(2.0)
@@ -290,7 +274,7 @@
         return pl.ds(pl.multiple_of(n * size, size), size)
 
     def score_block(kc, qc, t):
-        @pl.when(t == min(3, nx * nx - 1))
+        @pl.when(t == 1)
         def _():
             start_q(2)
             start_q(1)
@@ -347,19 +331,28 @@
     st[me_q] = rr[0:2, :]
     start_q(3)
 
+    xt[:, :, tok:] = jnp.zeros((npc, nzh * chunk, 256 - tok), bf16)
+    gr[:, tok:, :] = jnp.zeros((npc, 256 - tok, 384), bf16)
+    four = eye(4 * chunk)
+    for g in range(nzh * npc // 4):
+        turned = dot_nt(four, xb[:, g * 4 * chunk : (g + 1) * 4 * chunk]).astype(bf16)
+        for j in range(4):
+            n = 4 * g + j
+            rows = slice(n // npc * chunk, (n // npc + 1) * chunk)
+            xt[n % npc, rows, 0:tok] = turned[j * chunk : (j + 1) * chunk, :]
+
+    def x_block(s, n):
+        return send(xt.at[s], xr.at[n], x_send.at[s], x_recv.at[n], at_p(s))
+
+    own = pltpu.make_async_copy(xt.at[me_p], xr.at[me_p], own_sem)
+    own.start()
+
     def x_block(s, n):
         return send(xt.at[s], xr.at[n], x_send.at[s], x_recv.at[n], at_p(s))
 
     each(me_p, npc, lambda s: x_block(s, me_p).start())
     kt[...] = dot_nt(eye(128), kb[...]).astype(bf16)
     sweep((1, 2), grad_block)
-    wide = 512 if n_query % 512 == 0 else tq
-
-    @pl.loop(0, n_query // wide)
-    def _(t):
-        at = pl.ds(pl.multiple_of(t * wide, wide), wide)
-        dqt[:, at] = dot(kt[...], ut[:, at])
-
     for i in range(nzh):
         land_q(3, i)
 
@@ -371,15 +364,25 @@
         total = total + st[s, 1:2, :] * jnp.exp2((st[s, 0:1, :] - peak) * rate)
     rr[3:4, :] = jnp.exp2((rr[0:1, :] - peak) * rate) / total
 
-    def scale_rows(t):
+    @pl.loop(0, n_query // tq)
+    def _(t):
         at = tile(t)
-        factor = rr[3:4, at]
-        dqs[at, :] = jnp.transpose(dqt[:, at] * (factor * score_scale)).astype(bf16)
-        col = as_column(factor)
-        gs[at, :] = (gb[at, :].astype(f32) * col).astype(bf16)
-        qs[at, :] = (qb[at, :].astype(f32) * (col * score_scale)).astype(bf16)
-
-    pl.loop(0, n_query // tq)(scale_rows)
+        gs[at, :] = (gb[at, :].astype(f32) * as_column(rr[3:4, at])).astype(bf16)
+
+    def query_grads():
+        wide = 512 if n_query % 512 == 0 else tq
+
+        @pl.loop(0, n_query // wide)
+        def _(t):
+            at = pl.ds(pl.multiple_of(t * wide, wide), wide)
+            dqt[:, at] = dot(kt[...], ut[:, at])
+
+        @pl.loop(0, n_query // tq)
+        def _(t):
+            at = tile(t)
+            factor = rr[3:4, at] * score_scale
+            dqs[at, :] = jnp.transpose(dqt[:, at] * factor).astype(bf16)
+            qs[at, :] = (qb[at, :].astype(f32) * as_column(factor)).astype(bf16)
 
     def pair_block(w, core):
         src = dqs.at[rows_of(w * nc + core), :]
@@ -391,8 +394,6 @@
     def send_pair(w, carry):
         pair_block(w, other).start()
         return carry
-
-    lax.fori_loop(0, nz, send_pair, 0)
 
     def send_dq():
         def add(w):
@@ -419,7 +420,8 @@
         out, left, right = ((dks, ut, qs), (dvs, et, gs))[j]
 
         def step(i, carry):
-            t = lax.rem(x + 2 + i, nx)
+            last = nx - 1 - i
+            t = lax.rem(x + last + last // 2 - 2 * (last // 3), nx)
             at = pl.ds(pl.multiple_of(t * tb, tb), tb)
             out[at, :] = dot(left[at, :], right[...]).astype(bf16)
             for b in range(ny):
@@ -494,28 +496,30 @@
         wg[:, 128 * j : 128 * j + 128] = summed(ar.at[j])
         weight_out(j).start()
 
-    grad_tiles(1, 0, 1)
+    grad_tiles(1, 0, nx)
+    dvr[me_k] = dvs[mine_k, :]
+    query_grads()
+    lax.fori_loop(0, nz, send_pair, 0)
+    grad_tiles(0, 0, 1)
     send_dq()
-    grad_tiles(1, 1, nx)
-    dvr[me_k] = dvs[mine_k, :]
-    grad_tiles(0, 0, nx)
+    grad_tiles(0, 1, nx)
     dkr[me_k] = dks[mine_k, :]
+    each(me_k, nk, lambda s: kv_block(1, s, s).wait_recv())
+    send_grad(2, dvr)
+    own.wait()
+    each(me_p, npc, lambda s: x_block(s, s).wait_recv())
+    send_weight(2)
     each_z(lambda w: dq_block(w, w).wait_recv())
     send_grad(0, dqr)
-    own.wait()
-    each(me_p, npc, lambda s: x_block(s, s).wait_recv())
-    each(me_k, nk, lambda s: kv_block(1, s, s).wait_recv())
-    send_grad(2, dvr)
-    send_weight(0)
     each(me_k, nk, lambda s: kv_block(0, s, s).wait_recv())
     send_grad(1, dkr)
-    send_weight(2)
+    send_rows(2)
+    send_weight(0)
+    send_weight(1)
+    finish(2)
     send_rows(0)
-    send_weight(1)
-    send_rows(2)
+    send_rows(1)
     finish(0)
-    send_rows(1)
-    finish(2)
     finish(1)
 
     for m in range(4):

time: 100 us -> 102 us (1.020)
  Pallas kernels: 99.5 us -> 101 us
    pallas_call x1, Pallas kernels: 97.7 us -> 99.5 us  [local(): pl.pallas_call(body, out_shape=shapes, in_specs=[hbm] * 8, out_specs=(hbm...]
where the time goes in v6:
time: 102 us
  Pallas kernels  101 us (99%)
    pallas_call x1, Pallas kernels, local(): pl.pallas_call(body, out_shape=shapes, in_specs=[hbm] * 8, out_specs=(hbm...  99.5 us

profile of v6, /device:TPU:1, one launch (start us, length us, event | category | flops | bytes accessed | tf_op | source)
XLA Modules:
  0.0 101.8 jit_solution(10089634221563082933)
XLA Ops:
  0.6 99.5 %packed_backward.1 = (bf16[160,128]{1,0:T(8,128)(2,1)}, bf16[160,128]{1,0:T(8,128)(2,1)}, bf16[160,128]{1,0:T(8,128)(2,1)}, f32[96,384]{1,0:T(8,128)}) custom-call(bf16[160,128]{1,0:T(8,128)(2,1)} %refs_0_.1, bf16[160,128]{1,0:T(8,128)(2,1)} %refs_1_.1, bf16[160,128]{1,0:T(8,128)(2,1)} %refs_2_.1, bf16[160,128]{1,0:T(8,128)(2,1)} %refs_3_.1, ...), custom_call_target="tpu_custom_call" | custom-call | tf_op jit(solution)/shard_map/packed_backward/pallas_call | solution.py:620
  100.1 1.7 %hand_out.1 = (bf16[160,128]{1,0:T(8,128)(2,1)}, bf16[160,128]{1,0:T(8,128)(2,1)}, bf16[160,128]{1,0:T(8,128)(2,1)}, f32[96,384]{1,0:T(8,128)}) custom-call(bf16[160,128]{1,0:T(8,128)(2,1)} %get-tuple-element.8.refs_0_, bf16[160,128]{1,0:T(8,128)(2,1)} %get-tuple-element.9.refs_1_, bf16[160,128]{1,0:T(8,128)(2,1)} %get-tuple-element.10.refs_2_, ...), custom_call_target="tpu_custom_call" | custom-call | tf_op jit(solution)/shard_map/hand_out/pallas_call | solution.py:631

commit v7 on v5

--- a/solution.py
+++ b/solution.py
@@ -142,18 +142,24 @@
     def hello(device):
         pl.semaphore_signal(barrier, inc=1, device_id=device, device_id_type=MESH)
 
-    each(me_q, nq, lambda s: hello(at_z(s // nc, lax.rem(s, nc))))
-    each(me_k, nk, lambda s: hello(at_xy(s // ny, lax.rem(s, ny))))
-    each(me_p, npc, lambda s: hello(at_p(s)))
-    each(zh, nzh, lambda s: hello(at_zh(s)))
-    each(me_r, nr, lambda s: hello(at_r(s)))
+    each_z(lambda w: hello(at_z(w, c)))
+    hello(partner)
+    each_xy(lambda a, b: hello(at_xy(a, b)))
+    each_y(lambda b: hello((x, zl, zh, b, other)))
+
+    def across(a):
+        for n in range(1, nzl):
+            hello((a, lax.rem(zl + n, nzl), zh, y, c))
+
+    for n in range(1, nx):
+        across(lax.rem(x + n, nx))
 
     for copy in staged[:5]:
         copy.wait()
     product = gb[mine_q, :].astype(f32) * ob[...].astype(f32)
     delta = dot_nt(jnp.ones((8, product.shape[1]), f32), product, precision=lax.Precision.HIGHEST)
     db[me_q, :, 0:tok] = delta[0:1, :]
-    pl.semaphore_wait(barrier, nq + nk + npc + nzh + nr - 5)
+    pl.semaphore_wait(barrier, nz + nk + ny - 2 + (nx - 1) * (nzl - 1))
 
     def q_block(m, s, device, sem, n):
         ref = (qb.at[rows_of(s), :], gb.at[rows_of(s), :], db.at[s], st.at[s])[m]
@@ -500,6 +506,18 @@
     dvr[me_k] = dvs[mine_k, :]
     grad_tiles(0, 0, nx)
     dkr[me_k] = dks[mine_k, :]
+    for m in range(4):
+        each_z(lambda w: q_block(m, me_q, partner, q_send, w).wait_send())
+
+        def f_left(w, carry):
+            q_block(m, me_q, partner, f_send, w).wait_send()
+            return carry
+
+        lax.fori_loop(0, nz, f_left, 0)
+
+    for j in range(2):
+        each(me_k, nk, lambda s: k_block(j, me_k, partner, s).wait_send())
+
     each_z(lambda w: dq_block(w, w).wait_recv())
     send_grad(0, dqr)
     own.wait()
@@ -515,17 +533,6 @@
     send_rows(2)
     finish(0)
     send_rows(1)
-    finish(2)
-    finish(1)
-
-    for m in range(4):
-        each_z(lambda w: q_block(m, me_q, partner, q_send, w).wait_send())
-
-        def f_left(w, carry):
-            q_block(m, me_q, partner, f_send, w).wait_send()
-            return carry
-
-        lax.fori_loop(0, nz, f_left, 0)
 
     def pair_left(w, carry):
         pair_block(w, other).wait_send()
@@ -536,7 +543,6 @@
 
     def k_left(s):
         for j in range(2):
-            k_block(j, me_k, partner, s).wait_send()
             kv_block(j, s, me_k).wait_send()
 
     each(me_k, nk, k_left)
@@ -551,8 +557,12 @@
 
         lax.fori_loop(0, ny, h_left, 0)
         each(zh, nzh, lambda s: w_block(j, s, zh).wait_send())
+        grad_out(j).wait()
+
+    finish(2)
+    finish(1)
+    for j in range(3):
         each(me_r, nr, lambda s: a_block(j, s, me_r).wait_send())
-        grad_out(j).wait()
         weight_out(j).wait()
 
 

time: 100 us -> 99.9 us (level); the launches traced: 100 us -> 98.9 us
  Pallas kernels: 99.5 us -> 98.3 us
    pallas_call x1, Pallas kernels: 97.7 us -> 96.6 us  [local(): pl.pallas_call(body, out_shape=shapes, in_specs=[hbm] * 8, out_specs=(hbm...]
where the time goes in v7:
time: 99.9 us; the launch traced here: 98.9 us
  Pallas kernels  98.3 us (98%)
    pallas_call x1, Pallas kernels, local(): pl.pallas_call(body, out_shape=shapes, in_specs=[hbm] * 8, out_specs=(hbm...  96.6 us

profile of v7, /device:TPU:1, one launch (start us, length us, event | category | flops | bytes accessed | tf_op | source)
XLA Modules:
  0.0 98.9 jit_solution(13725211259196909891)
XLA Ops:
  0.6 96.6 %packed_backward.1 = (bf16[160,128]{1,0:T(8,128)(2,1)}, bf16[160,128]{1,0:T(8,128)(2,1)}, bf16[160,128]{1,0:T(8,128)(2,1)}, f32[96,384]{1,0:T(8,128)}) custom-call(bf16[160,128]{1,0:T(8,128)(2,1)} %refs_0_.1, bf16[160,128]{1,0:T(8,128)(2,1)} %refs_1_.1, bf16[160,128]{1,0:T(8,128)(2,1)} %refs_2_.1, bf16[160,128]{1,0:T(8,128)(2,1)} %refs_3_.1, ...), custom_call_target="tpu_custom_call" | custom-call | tf_op jit(solution)/shard_map/packed_backward/pallas_call | solution.py:626
  97.2 1.7 %hand_out.1 = (bf16[160,128]{1,0:T(8,128)(2,1)}, bf16[160,128]{1,0:T(8,128)(2,1)}, bf16[160,128]{1,0:T(8,128)(2,1)}, f32[96,384]{1,0:T(8,128)}) custom-call(bf16[160,128]{1,0:T(8,128)(2,1)} %get-tuple-element.8.refs_0_, bf16[160,128]{1,0:T(8,128)(2,1)} %get-tuple-element.9.refs_1_, bf16[160,128]{1,0:T(8,128)(2,1)} %get-tuple-element.10.refs_2_, ...), custom_call_target="tpu_custom_call" | custom-call | tf_op jit(solution)/shard_map/hand_out/pallas_call | solution.py:637

commit v8 on v7

--- a/solution.py
+++ b/solution.py
@@ -474,10 +474,13 @@
             g_block(j, b * nc + other, partner, h_send, b).wait_recv()
             return carry
 
+        def terms(core):
+            parts = [b * nc + core for b in range(ny)]
+            return sum(dot(xr[p], gr[p, :, 128 * j : 128 * j + 128]) for p in parts)
+
+        acc = terms(c)
         lax.fori_loop(0, ny, land_rest, 0)
-        acc = dot(xr[0], gr[0, :, 128 * j : 128 * j + 128])
-        for p in range(1, npc):
-            acc = acc + dot(xr[p], gr[p, :, 128 * j : 128 * j + 128])
+        acc = acc + terms(other)
         for n in range(nzh):
             ws[j, n] = acc[n * chunk : (n + 1) * chunk, :].astype(bf16)
         each(zh, nzh, lambda s: w_block(j, s, zh).start())

time: 99.9 us -> 99.5 us (level)
  no operation moved by 1% of the time
where the time goes in v8:
time: 99.5 us; the launch traced here: 99.1 us
  Pallas kernels  98.4 us (99%)
    pallas_call x1, Pallas kernels, local(): pl.pallas_call(body, out_shape=shapes, in_specs=[hbm] * 8, out_specs=(hbm...  96.7 us

profile of v8, /device:TPU:1, one launch (start us, length us, event | category | flops | bytes accessed | tf_op | source)
XLA Modules:
  0.0 99.1 jit_solution(113687010844453426)
XLA Ops:
  0.6 96.7 %packed_backward.1 = (bf16[160,128]{1,0:T(8,128)(2,1)}, bf16[160,128]{1,0:T(8,128)(2,1)}, bf16[160,128]{1,0:T(8,128)(2,1)}, f32[96,384]{1,0:T(8,128)}) custom-call(bf16[160,128]{1,0:T(8,128)(2,1)} %refs_0_.1, bf16[160,128]{1,0:T(8,128)(2,1)} %refs_1_.1, bf16[160,128]{1,0:T(8,128)(2,1)} %refs_2_.1, bf16[160,128]{1,0:T(8,128)(2,1)} %refs_3_.1, ...), custom_call_target="tpu_custom_call" | custom-call | tf_op jit(solution)/shard_map/packed_backward/pallas_call | solution.py:629
  97.4 1.7 %hand_out.1 = (bf16[160,128]{1,0:T(8,128)(2,1)}, bf16[160,128]{1,0:T(8,128)(2,1)}, bf16[160,128]{1,0:T(8,128)(2,1)}, f32[96,384]{1,0:T(8,128)}) custom-call(bf16[160,128]{1,0:T(8,128)(2,1)} %get-tuple-element.8.refs_0_, bf16[160,128]{1,0:T(8,128)(2,1)} %get-tuple-element.9.refs_1_, bf16[160,128]{1,0:T(8,128)(2,1)} %get-tuple-element.10.refs_2_, ...), custom_call_target="tpu_custom_call" | custom-call | tf_op jit(solution)/shard_map/hand_out/pallas_call | solution.py:640
